TPU v7x, 32 devices: a whole 2x2x4 slice. The times are simulated.
32 devices in a mesh: row: 8 (over z, core), col: 4 (over y, x).
Axes of the slice: x: 2, y: 2, z: 4, core: 2. Of those that a mesh axis runs over, the one named last changes fastest.
Arguments:
- features: bfloat16 [8, 4, 1024, 602], P('row', 'col'), may hold values from -6 to 6
- local_mask: int32 [8, 4, 1024, 1024], P('row', 'col'), may hold values 0 or 1
- halo_mask: int32 [8, 4, 1024, 512], P('row', 'col'), may hold values 0 or 1
- boundary_index: int32 [8, 4, 512], P('row', 'col'), may hold values from 0 to 1023
- labels: int32 [8, 4, 1024], P('row', 'col'), may hold values from 0 to 40
- halo_first: bfloat16 [8, 4, 512, 602], P('row', 'col'), may hold values from -6 to 6
- halo_second: bfloat16 [8, 4, 512, 256], P('row', 'col'), may hold values from -4 to 4
- halo_third: bfloat16 [8, 4, 512, 256], P('row', 'col'), may hold values from -4 to 4
- return_second: bfloat16 [8, 4, 512, 256], P('row', 'col'), may hold values from -0.0059814453 to 0.0059814453
- return_third: bfloat16 [8, 4, 512, 256], P('row', 'col'), may hold values from -0.0059814453 to 0.0059814453
- weight_first: bfloat16 [602, 256], replicated, may hold values from -1 to 1
- weight_second: bfloat16 [256, 256], replicated, may hold values from -1.5 to 1.5
- weight_third: bfloat16 [256, 41], replicated, may hold values from -1.5 to 1.5
Outputs:
- grad_first: float32 [602, 256], replicated
- grad_second: float32 [256, 256], replicated
- grad_third: float32 [256, 41], replicated
- next_second: bfloat16 [8, 4, 512, 256], P('row', 'col')
- next_third: bfloat16 [8, 4, 512, 256], P('row', 'col')
- back_second: bfloat16 [8, 4, 512, 256], P('row', 'col')
- back_third: bfloat16 [8, 4, 512, 256], P('row', 'col')
All inputs are finite; a program needn't handle non-finite values. No bound on the sum of `local_mask` or of `halo_mask` on one device may be relied on, other than what follows from the above.
Results may differ from a plain program's by a relative error of at most 0.007.
Values may be sent and summed in bfloat16 or wider, within the bound.
A program may use at most 64 MiB of HBM per device.

v0:
```python
import jax
import jax.numpy as jnp
from jax import lax
from jax.sharding import PartitionSpec as P


def padded(shard, sides, width):
    for axis, dim in sides:
        size, length = (lax.axis_size(axis), shard.shape[dim])
        up = [(i, (i + 1) % size) for i in range(size - 1)]
        down = [(j, i) for i, j in up]
        last = lax.slice_in_dim(shard, length - width, length, axis=dim)
        initial = lax.slice_in_dim(shard, 0, width, axis=dim)
        before = lax.ppermute(last, axis, up)
        after = lax.ppermute(initial, axis, down)
        shard = jnp.concatenate([before, shard, after], axis=dim)
    return shard


def slope(pre):
    sigma = jax.nn.sigmoid(pre)
    return sigma * (1.0 + pre * (1.0 - sigma))


def spread(local_bf, halo_bf, inverse, values, remote):
    summed = jnp.dot(local_bf, values, preferred_element_type=jnp.float32)
    summed = summed + values.astype(jnp.float32)
    summed = summed + jnp.dot(halo_bf, remote, preferred_element_type=jnp.float32)
    return (summed * inverse).astype(jnp.bfloat16)


def retract(local_bf, halo_bf, inverse, upstream, weight, hits, returned):
    across = jnp.dot(upstream, weight.T, preferred_element_type=jnp.float32)
    scaled = (across * inverse).astype(jnp.bfloat16)
    carried = jnp.dot(local_bf.T, scaled, preferred_element_type=jnp.float32) + scaled.astype(
        jnp.float32
    )
    carried = carried + jnp.dot(hits, returned, preferred_element_type=jnp.float32)
    outgoing = jnp.dot(halo_bf.T, scaled, preferred_element_type=jnp.float32).astype(jnp.bfloat16)
    return (carried, outgoing)


def arrange(vertical, lateral, shape):
    joined = jnp.concatenate([vertical[0:1], vertical[3:4], lateral[0:1], lateral[3:4]], axis=0)
    return joined.reshape(shape)[None, None]


def trade_features(sent):
    parted = sent.reshape((4, sent.shape[0] // 4, sent.shape[1]))
    vertical = padded(parted[0:2], (("row", 0),), 1)
    lateral = padded(parted[2:4], (("col", 0),), 1)
    return arrange(vertical, lateral, sent.shape)


def trade_gradients(sent):
    parted = sent.reshape((4, sent.shape[0] // 4, sent.shape[1]))
    vertical = padded(parted[0:2], (("row", 0),), 1)
    lateral = padded(parted[2:4], (("col", 0),), 1)
    return arrange(vertical, lateral, sent.shape)


def per_device(
    features,
    local_mask,
    halo_mask,
    boundary_index,
    labels,
    halo_first,
    halo_second,
    halo_third,
    return_second,
    return_third,
    weight_first,
    weight_second,
    weight_third,
):
    features = features[0, 0]
    local_mask = local_mask[0, 0]
    halo_mask = halo_mask[0, 0]
    boundary_index = boundary_index[0, 0]
    labels = labels[0, 0]
    local_bf = local_mask.astype(jnp.bfloat16)
    halo_bf = halo_mask.astype(jnp.bfloat16)
    degree = (
        1.0
        + jnp.sum(local_mask, axis=1).astype(jnp.float32)
        + jnp.sum(halo_mask, axis=1).astype(jnp.float32)
    )
    inverse = (1.0 / degree)[:, None]
    node_rows = features.shape[0]
    hits = (jnp.arange(node_rows, dtype=jnp.int32)[:, None] == boundary_index[None, :]).astype(
        jnp.bfloat16
    )
    mixed_one = spread(local_bf, halo_bf, inverse, features, halo_first[0, 0])
    pre_one = jnp.dot(mixed_one, weight_first, preferred_element_type=jnp.float32)
    hidden_one = jax.nn.silu(pre_one).astype(jnp.bfloat16)
    next_second = trade_features(jnp.take(hidden_one, boundary_index, axis=0))
    mixed_two = spread(local_bf, halo_bf, inverse, hidden_one, halo_second[0, 0])
    pre_two = jnp.dot(mixed_two, weight_second, preferred_element_type=jnp.float32)
    hidden_two = jax.nn.silu(pre_two).astype(jnp.bfloat16)
    next_third = trade_features(jnp.take(hidden_two, boundary_index, axis=0))
    mixed_three = spread(local_bf, halo_bf, inverse, hidden_two, halo_third[0, 0])
    logits = jnp.dot(mixed_three, weight_third, preferred_element_type=jnp.float32)
    expo = jnp.exp(logits)
    probs = expo / jnp.sum(expo, axis=1, keepdims=True)
    target = (labels[:, None] == jnp.arange(logits.shape[1], dtype=jnp.int32)[None, :]).astype(
        jnp.float32
    )
    upstream_three = ((probs - target) / node_rows).astype(jnp.bfloat16)
    grad_three = jnp.dot(mixed_three.T, upstream_three, preferred_element_type=jnp.float32)
    carried_two, outgoing_three = retract(
        local_bf, halo_bf, inverse, upstream_three, weight_third, hits, return_third[0, 0]
    )
    back_third = trade_gradients(outgoing_three)
    upstream_two = (carried_two * slope(pre_two)).astype(jnp.bfloat16)
    grad_two = jnp.dot(mixed_two.T, upstream_two, preferred_element_type=jnp.float32)
    carried_one, outgoing_two = retract(
        local_bf, halo_bf, inverse, upstream_two, weight_second, hits, return_second[0, 0]
    )
    back_second = trade_gradients(outgoing_two)
    upstream_one = (carried_one * slope(pre_one)).astype(jnp.bfloat16)
    grad_one = jnp.dot(mixed_one.T, upstream_one, preferred_element_type=jnp.float32)
    grad_one, grad_two, grad_three = lax.psum((grad_one, grad_two, grad_three), ("row", "col"))
    return (grad_one, grad_two, grad_three, next_second, next_third, back_second, back_third)


def solution(mesh):
    placed = (
        P("row", "col", None, None),
        P("row", "col", None, None),
        P("row", "col", None, None),
        P("row", "col", None),
        P("row", "col", None),
        P("row", "col", None, None),
        P("row", "col", None, None),
        P("row", "col", None, None),
        P("row", "col", None, None),
        P("row", "col", None, None),
        P(),
        P(),
        P(),
    )
    return jax.shard_map(
        per_device,
        mesh=mesh,
        in_specs=placed,
        out_specs=(
            P(),
            P(),
            P(),
            P("row", "col", None, None),
            P("row", "col", None, None),
            P("row", "col", None, None),
            P("row", "col", None, None),
        ),
        check_vma=False,
    )
```

profile of v0, /device:TPU:0, one launch (start us, length us, event | category | flops | bytes accessed | tf_op | source)
XLA Modules:
  0.0 201.1 jit_solution(8353435630953365775)
XLA Ops:
  7.2 0.7 compare_and_fusion
  8.0 0.7 compare_select_fusion
  8.7 2.6 %fusion.74 = (bf16[1,1,1024,512]{3,2,1,0:T(8,128)(2,1)S(1)}, s32[1024]{0:T(1024)S(1)}) fusion(s32[1,1,1024,512]{3,2,1,0:T(8,128)} %param.17), kind=kLoop, calls=%fused_computation.99 | loop fusion | flops 1047552 | bytes 3149824 | tf_op jit(solution)/shard_map/convert_element_type | solution.py:83
  11.3 4.3 %fusion.73 = (s32[1024]{0:T(1024)S(1)}, bf16[1,1,1024,1024]{3,2,1,0:T(8,128)(2,1)S(1)}) fusion(s32[1,1,1024,1024]{3,2,1,0:T(8,128)} %param.16), kind=kLoop, calls=%fused_computation.98 | loop fusion | flops 2096128 | bytes 6295552 | tf_op jit(solution)/shard_map/reduce_sum | solution.py:86
  15.6 1.5 fusion.8
  17.1 0.9 multiply_convert_fusion
  18.1 1.6 multiply_convert_fusion.2
  19.7 1.7 fusion.36
  21.4 1.9 gather_fusion
  23.4 1.7 fusion.43
  25.1 1.4 multiply_convert_fusion.1
  26.4 1.9 gather_fusion.1
  28.4 0.8 broadcast_select_fusion
  29.2 0.7 slice_bitcast_fusion.11
  29.9 3.1 %collective-permute-start.4 = (bf16[1,128,256]{2,1,0:T(8,128)(2,1)}, bf16[1,128,256]{2,1,0:T(8,128)(2,1)}, u32[]{:S(2)}, u32[]{:S(2)}) collective-permute-start(bf16[1,128,256]{2,1,0:T(8,128)(2,1)} %get-tuple-element.22), channel_id=1, source_target_pairs={{0,4},{4,8},{8,12},{12,16},{16,20},{20,24},{24,28},{1,5},{5,9},{9,... | collective-permute-start | bytes 196616 | tf_op jit(solution)/shard_map/ppermute | solution.py:14
  33.1 2.3 %fusion.39 = f32[1024,256]{1,0:T(8,128)S(1)} fusion(bf16[1024,256]{1,0:T(8,128)(2,1)S(1)} %get-tuple-element.34, bf16[1,1,1024,1024]{3,2,1,0:T(8,128)(2,1)} %copy-done.1), kind=kOutput, calls=%fused_computation.33 | convolution fusion | flops 537395200 | bytes 3670016 | tf_op jit(solution)/shard_map/dot_general | solution.py:26
  37.9 0.7 slice_bitcast_fusion.3
  38.6 4.7 %collective-permute-start.12 = (bf16[1,128,256]{1,2,0:T(8,128)(2,1)}, bf16[1,128,256]{1,2,0:T(8,128)(2,1)}, u32[]{:S(2)}, u32[]{:S(2)}) collective-permute-start(bf16[1,128,256]{1,2,0:T(8,128)(2,1)} %get-tuple-element.14), channel_id=1, source_target_pairs={{0,4},{4,8},{8,12},{12,16},{16,20},{20,24},{24,28},{1,5},{5,9},{9,... | collective-permute-start | bytes 196616 | tf_op jit(solution)/shard_map/ppermute | solution.py:14
  43.4 1.3 collective-permute-start.15
  44.6 5.2 %collective-permute-start.14 = (bf16[1,128,256]{1,2,0:T(8,128)(2,1)}, bf16[1,128,256]{1,2,0:T(8,128)(2,1)}, u32[]{:S(2)}, u32[]{:S(2)}) collective-permute-start(bf16[1,128,256]{1,2,0:T(8,128)(2,1)} %get-tuple-element.16), channel_id=1, source_target_pairs={{0,1},{1,2},{2,3},{4,5},{5,6},{6,7},{8,9},{9,10},{10,11},{12,13},{... | collective-permute-start | bytes 196616 | tf_op jit(solution)/shard_map/ppermute | solution.py:14
  49.8 1.5 collective-permute-start.13
  51.3 1.0 fusion.33
  52.3 0.8 fusion.46
  53.0 1.0 fusion.76
  54.4 1.9 fusion.30
  56.4 3.7 %fusion.49 = f32[602,256]{1,0:T(8,128)} fusion(bf16[1024,602]{0,1:T(8,128)(2,1)S(1)} %copy-done.5, f32[1024,256]{1,0:T(8,128)} %fusion.30, f32[1024,256]{1,0:T(8,128)} %get-tuple-element.33, s32[512]{0:T(512)S(1)} %bitcast.142, bf16[1,1,512,256]{3,2,1,0:T(8,128)(2,1)} %param.23), kind=kOutput, calls=%fused_computation.41 | convolution fusion | flops 587202560 | bytes 4210688 | tf_op jit(solution)/shard_map/dot_general | solution.py:122
  60.2 1.2 fusion.72
  61.9 40.9 %psum.23 = f32[256,41]{0,1:T(8,128)} all-reduce(f32[256,41]{0,1:T(8,128)S(1)} %fusion.72), channel_id=1, replica_groups=mesh['row'=8,'col'=4] {'row','col'}, use_global_device_ids=true, to_apply=%region_5.6 | all-reduce | flops 10496 | bytes 83968 | tf_op jit(solution)/shard_map/psum | solution.py:123
  102.8 1.3 collective-permute-start.8
  104.2 1.3 collective-permute-start.11
  105.5 4.8 %collective-permute-start.10 = (bf16[1,128,256]{1,2,0:T(8,128)(2,1)S(1)}, bf16[1,128,256]{1,2,0:T(8,128)(2,1)S(1)}, u32[]{:S(2)}, u32[]{:S(2)}) collective-permute-start(bf16[1,128,256]{1,2,0:T(8,128)(2,1)S(1)} %get-tuple-element.20), channel_id=1, source_target_pairs={{0,1},{1,2},{2,3},{4,5},{5,6},{6,7},{8,9},{9,10},{10,11},{12,13},{... | collective-permute-start | bytes 196616 | tf_op jit(solution)/shard_map/ppermute | solution.py:14
  110.3 1.3 collective-permute-start.9
  111.6 1.0 pad_maximum_fusion.3
  112.6 0.9 copy.27
  113.4 1.3 collective-permute-start.7
  114.7 5.4 %collective-permute-start.6 = (bf16[1,128,256]{2,1,0:T(8,128)(2,1)S(1)}, bf16[1,128,256]{2,1,0:T(8,128)(2,1)S(1)}, u32[]{:S(2)}, u32[]{:S(2)}) collective-permute-start(bf16[1,128,256]{2,1,0:T(8,128)(2,1)S(1)} %copy-done.13), channel_id=1, source_target_pairs={{0,1},{1,2},{2,3},{4,5},{5,6},{6,7},{8,9},{9,10},{10,11},{12,13},{... | collective-permute-start | bytes 196616 | tf_op jit(solution)/shard_map/ppermute | solution.py:14
  120.2 1.3 collective-permute-start.5
  121.5 3.9 %collective-permute-start = (bf16[1,128,256]{2,1,0:T(8,128)(2,1)S(1)}, bf16[1,128,256]{2,1,0:T(8,128)(2,1)S(1)}, u32[]{:S(2)}, u32[]{:S(2)}) collective-permute-start(bf16[1,128,256]{2,1,0:T(8,128)(2,1)S(1)} %get-tuple-element.26), channel_id=1, source_target_pairs={{0,4},{4,8},{8,12},{12,16},{16,20},{20,24},{24,28},{1,5},{5,9},{9,... | collective-permute-start | bytes 196616 | tf_op jit(solution)/shard_map/ppermute | solution.py:14
  125.4 0.9 copy.26
  126.3 1.3 collective-permute-start.3
  127.6 5.2 %collective-permute-start.2 = (bf16[1,128,256]{2,1,0:T(8,128)(2,1)S(1)}, bf16[1,128,256]{2,1,0:T(8,128)(2,1)S(1)}, u32[]{:S(2)}, u32[]{:S(2)}) collective-permute-start(bf16[1,128,256]{2,1,0:T(8,128)(2,1)S(1)} %get-tuple-element.28), channel_id=1, source_target_pairs={{0,1},{1,2},{2,3},{4,5},{5,6},{6,7},{8,9},{9,10},{10,11},{12,13},{... | collective-permute-start | bytes 196616 | tf_op jit(solution)/shard_map/ppermute | solution.py:14
  132.8 1.3 collective-permute-start.1
  134.1 1.6 pad_maximum_fusion.1
  135.7 1.8 collective-permute-done.1
  137.4 0.7 pad_maximum_fusion
  138.2 52.5 %all-reduce.3.cloned.1.call-done = (f32[602,256]{1,0:T(8,128)}, f32[256,256]{1,0:T(8,128)}) async-done(((f32[602,256]{1,0:T(8,128)}, f32[256,256]{1,0:T(8,128)}), (f32[602,256]{1,0:T(8,128)}, f32[256,256]{1,0:T(8,128)})) %all-reduce.3.cloned.1.call-update) | async-done | bytes 878608 | tf_op jit(solution)/shard_map/psum | solution.py:123
  190.7 1.9 copy.33
  192.6 1.7 copy.34
  (70 shorter events, 3.6 us)
Async XLA Ops:
  7.2 10.0 %copy-start = (bf16[1,1,512,602]{2,3,1,0:T(8,128)(2,1)S(1)}, bf16[1,1,512,602]{2,3,1,0:T(8,128)(2,1)}, u32[]{:S(2)}) copy-start(bf16[1,1,512,602]{2,3,1,0:T(8,128)(2,1)} %param.20) | copy-start | bytes 1849348
  7.2 183.5 %all-reduce.3.cloned.1.call-start = ((), (), s32[]{:S(2)}) async-start(), calls=%async_computation | async-start | bytes 1769472 | tf_op jit(solution)/shard_map/psum | solution.py:123
  11.3 4.3 %copy-start.3 = (bf16[1,1,1024,602]{2,3,1,0:T(8,128)(2,1)S(1)}, bf16[1,1,1024,602]{2,3,1,0:T(8,128)(2,1)}, u32[]{:S(2)}) copy-start(bf16[1,1,1024,602]{2,3,1,0:T(8,128)(2,1)} %param.15) | copy-start | bytes 3698692
  15.6 4.1 %copy-start.1 = (bf16[1,1,1024,1024]{3,2,1,0:T(8,128)(2,1)}, bf16[1,1,1024,1024]{3,2,1,0:T(8,128)(2,1)S(1)}, u32[]{:S(2)}) copy-start(bf16[1,1,1024,1024]{3,2,1,0:T(8,128)(2,1)S(1)} %get-tuple-element.11) | copy-start | bytes 6291460
  17.1 1.0 copy-start.17
  18.1 1.6 copy-start.4
  21.4 2.0 copy-start.9
  21.4 3.6 %copy-start.12 = (bf16[256,256]{1,0:T(8,128)(2,1)S(1)}, bf16[256,256]{1,0:T(8,128)(2,1)}, u32[]{:S(2)}) copy-start(bf16[256,256]{1,0:T(8,128)(2,1)} %param.26) | copy-start | bytes 393220
  29.9 5.5 %copy-start.10 = (bf16[1,1,512,256]{3,2,1,0:T(8,128)(2,1)S(1)}, bf16[1,1,512,256]{3,2,1,0:T(8,128)(2,1)}, u32[]{:S(2)}) copy-start(bf16[1,1,512,256]{3,2,1,0:T(8,128)(2,1)} %param.22) | copy-start | bytes 786436
  29.9 96.4 %collective-permute-start.4 = (bf16[1,128,256]{2,1,0:T(8,128)(2,1)}, bf16[1,128,256]{2,1,0:T(8,128)(2,1)}, u32[]{:S(2)}, u32[]{:S(2)}) collective-permute-start(bf16[1,128,256]{2,1,0:T(8,128)(2,1)} %get-tuple-element.22), channel_id=1, source_target_pairs={{0,4},{4,8},{8,12},{12,16},{16,20},{20,24},{24,28},{1,5},{5,9},{9,... | collective-permute-start | bytes 196616 | tf_op jit(solution)/shard_map/ppermute | solution.py:14
  35.4 0.7 copy-start.15
  35.4 1.7 copy-start.19
  36.4 0.7 copy-start.11
  36.4 14.9 %copy-start.2 = (bf16[1,1,1024,1024]{3,2,1,0:T(8,128)(2,1)S(1)}, bf16[1,1,1024,1024]{3,2,1,0:T(8,128)(2,1)}, u32[]{:S(2)}) copy-start(bf16[1,1,1024,1024]{3,2,1,0:T(8,128)(2,1)} %copy-done.1) | copy-start | bytes 6291460
  38.6 13.6 %copy-start.16 = (s32[1,1,512]{2,1,0:T(1,128)S(1)}, s32[1,1,512]{2,1,0:T(1,128)}, u32[]{:S(2)}) copy-start(s32[1,1,512]{2,1,0:T(1,128)} %param.18) | copy-start | bytes 6148
  38.6 13.6 %copy-start.18 = (bf16[1,1,512,256]{3,2,1,0:T(8,128)(2,1)S(1)}, bf16[1,1,512,256]{3,2,1,0:T(8,128)(2,1)}, u32[]{:S(2)}) copy-start(bf16[1,1,512,256]{3,2,1,0:T(8,128)(2,1)} %param.24) | copy-start | bytes 786436
  38.6 13.6 %copy-start.20 = (f32[1024,256]{1,0:T(8,128)S(1)}, f32[1024,256]{1,0:T(8,128)}, u32[]{:S(2)}) copy-start(f32[1024,256]{1,0:T(8,128)} %get-tuple-element.35) | copy-start | bytes 3145732
  38.6 64.2 %collective-permute-start.12 = (bf16[1,128,256]{1,2,0:T(8,128)(2,1)}, bf16[1,128,256]{1,2,0:T(8,128)(2,1)}, u32[]{:S(2)}, u32[]{:S(2)}) collective-permute-start(bf16[1,128,256]{1,2,0:T(8,128)(2,1)} %get-tuple-element.14), channel_id=1, source_target_pairs={{0,4},{4,8},{8,12},{12,16},{16,20},{20,24},{24,28},{1,5},{5,9},{9,... | collective-permute-start | bytes 196616 | tf_op jit(solution)/shard_map/ppermute | solution.py:14
  43.4 60.8 %collective-permute-start.15 = (bf16[1,128,256]{1,2,0:T(8,128)(2,1)}, bf16[1,128,256]{1,2,0:T(8,128)(2,1)}, u32[]{:S(2)}, u32[]{:S(2)}) collective-permute-start(bf16[1,128,256]{1,2,0:T(8,128)(2,1)} %get-tuple-element.15), channel_id=1, source_target_pairs={{1,0},{2,1},{3,2},{5,4},{6,5},{7,6},{9,8},{10,9},{11,10},{13,12},{... | collective-permute-start | bytes 196616 | tf_op jit(solution)/shard_map/ppermute | solution.py:15
  44.6 60.9 %collective-permute-start.14 = (bf16[1,128,256]{1,2,0:T(8,128)(2,1)}, bf16[1,128,256]{1,2,0:T(8,128)(2,1)}, u32[]{:S(2)}, u32[]{:S(2)}) collective-permute-start(bf16[1,128,256]{1,2,0:T(8,128)(2,1)} %get-tuple-element.16), channel_id=1, source_target_pairs={{0,1},{1,2},{2,3},{4,5},{5,6},{6,7},{8,9},{9,10},{10,11},{12,13},{... | collective-permute-start | bytes 196616 | tf_op jit(solution)/shard_map/ppermute | solution.py:14
  49.8 60.5 %collective-permute-start.13 = (bf16[1,128,256]{1,2,0:T(8,128)(2,1)}, bf16[1,128,256]{1,2,0:T(8,128)(2,1)}, u32[]{:S(2)}, u32[]{:S(2)}) collective-permute-start(bf16[1,128,256]{1,2,0:T(8,128)(2,1)} %get-tuple-element.17), channel_id=1, source_target_pairs={{4,0},{8,4},{12,8},{16,12},{20,16},{24,20},{28,24},{5,1},{9,5},{13... | collective-permute-start | bytes 196616 | tf_op jit(solution)/shard_map/ppermute | solution.py:15
  54.4 2.0 copy-start.7
  54.4 1.9 copy-start.5
  60.1 1.2 copy-start.8
  60.1 1.7 copy-start.6
  61.4 52.1 %copy-start.14 = (bf16[1,128,256]{2,1,0:T(8,128)(2,1)S(1)}, bf16[1,128,256]{2,1,0:T(8,128)(2,1)}, u32[]{:S(2)}) copy-start(bf16[1,128,256]{2,1,0:T(8,128)(2,1)} %get-tuple-element.23) | copy-start | bytes 196612
  61.4 53.3 %copy-start.13 = (bf16[1,128,256]{2,1,0:T(8,128)(2,1)S(1)}, bf16[1,128,256]{2,1,0:T(8,128)(2,1)}, u32[]{:S(2)}) copy-start(bf16[1,128,256]{2,1,0:T(8,128)(2,1)} %get-tuple-element.24) | copy-start | bytes 196612
  102.8 10.6 %collective-permute-start.8 = (bf16[1,128,256]{1,2,0:T(8,128)(2,1)S(1)}, bf16[1,128,256]{1,2,0:T(8,128)(2,1)S(1)}, u32[]{:S(2)}, u32[]{:S(2)}) collective-permute-start(bf16[1,128,256]{1,2,0:T(8,128)(2,1)S(1)} %get-tuple-element.18), channel_id=1, source_target_pairs={{0,4},{4,8},{8,12},{12,16},{16,20},{20,24},{24,28},{1,5},{5,9},{9,... | collective-permute-start | bytes 196616 | tf_op jit(solution)/shard_map/ppermute | solution.py:14
  104.2 10.5 %collective-permute-start.11 = (bf16[1,128,256]{1,2,0:T(8,128)(2,1)S(1)}, bf16[1,128,256]{1,2,0:T(8,128)(2,1)S(1)}, u32[]{:S(2)}, u32[]{:S(2)}) collective-permute-start(bf16[1,128,256]{1,2,0:T(8,128)(2,1)S(1)} %get-tuple-element.19), channel_id=1, source_target_pairs={{1,0},{2,1},{3,2},{5,4},{6,5},{7,6},{9,8},{10,9},{11,10},{13,12},{... | collective-permute-start | bytes 196616 | tf_op jit(solution)/shard_map/ppermute | solution.py:15
  105.5 14.7 %collective-permute-start.10 = (bf16[1,128,256]{1,2,0:T(8,128)(2,1)S(1)}, bf16[1,128,256]{1,2,0:T(8,128)(2,1)S(1)}, u32[]{:S(2)}, u32[]{:S(2)}) collective-permute-start(bf16[1,128,256]{1,2,0:T(8,128)(2,1)S(1)} %get-tuple-element.20), channel_id=1, source_target_pairs={{0,1},{1,2},{2,3},{4,5},{5,6},{6,7},{8,9},{9,10},{10,11},{12,13},{... | collective-permute-start | bytes 196616 | tf_op jit(solution)/shard_map/ppermute | solution.py:14
  110.3 11.2 %collective-permute-start.9 = (bf16[1,128,256]{1,2,0:T(8,128)(2,1)S(1)}, bf16[1,128,256]{1,2,0:T(8,128)(2,1)S(1)}, u32[]{:S(2)}, u32[]{:S(2)}) collective-permute-start(bf16[1,128,256]{1,2,0:T(8,128)(2,1)S(1)} %get-tuple-element.21), channel_id=1, source_target_pairs={{4,0},{8,4},{12,8},{16,12},{20,16},{24,20},{28,24},{5,1},{9,5},{13... | collective-permute-start | bytes 196616 | tf_op jit(solution)/shard_map/ppermute | solution.py:15
  113.4 14.2 %collective-permute-start.7 = (bf16[1,128,256]{2,1,0:T(8,128)(2,1)S(1)}, bf16[1,128,256]{2,1,0:T(8,128)(2,1)S(1)}, u32[]{:S(2)}, u32[]{:S(2)}) collective-permute-start(bf16[1,128,256]{2,1,0:T(8,128)(2,1)S(1)} %copy-done.14), channel_id=1, source_target_pairs={{1,0},{2,1},{3,2},{5,4},{6,5},{7,6},{9,8},{10,9},{11,10},{13,12},{... | collective-permute-start | bytes 196616 | tf_op jit(solution)/shard_map/ppermute | solution.py:15
  114.7 18.0 %collective-permute-start.6 = (bf16[1,128,256]{2,1,0:T(8,128)(2,1)S(1)}, bf16[1,128,256]{2,1,0:T(8,128)(2,1)S(1)}, u32[]{:S(2)}, u32[]{:S(2)}) collective-permute-start(bf16[1,128,256]{2,1,0:T(8,128)(2,1)S(1)} %copy-done.13), channel_id=1, source_target_pairs={{0,1},{1,2},{2,3},{4,5},{5,6},{6,7},{8,9},{9,10},{10,11},{12,13},{... | collective-permute-start | bytes 196616 | tf_op jit(solution)/shard_map/ppermute | solution.py:14
  120.2 13.9 %collective-permute-start.5 = (bf16[1,128,256]{2,1,0:T(8,128)(2,1)S(1)}, bf16[1,128,256]{2,1,0:T(8,128)(2,1)S(1)}, u32[]{:S(2)}, u32[]{:S(2)}) collective-permute-start(bf16[1,128,256]{2,1,0:T(8,128)(2,1)S(1)} %get-tuple-element.25), channel_id=1, source_target_pairs={{4,0},{8,4},{12,8},{16,12},{20,16},{24,20},{28,24},{5,1},{9,5},{13... | collective-permute-start | bytes 196616 | tf_op jit(solution)/shard_map/ppermute | solution.py:15
  121.5 14.2 %collective-permute-start = (bf16[1,128,256]{2,1,0:T(8,128)(2,1)S(1)}, bf16[1,128,256]{2,1,0:T(8,128)(2,1)S(1)}, u32[]{:S(2)}, u32[]{:S(2)}) collective-permute-start(bf16[1,128,256]{2,1,0:T(8,128)(2,1)S(1)} %get-tuple-element.26), channel_id=1, source_target_pairs={{0,4},{4,8},{8,12},{12,16},{16,20},{20,24},{24,28},{1,5},{5,9},{9,... | collective-permute-start | bytes 196616 | tf_op jit(solution)/shard_map/ppermute | solution.py:14
  126.3 9.4 %collective-permute-start.3 = (bf16[1,128,256]{2,1,0:T(8,128)(2,1)S(1)}, bf16[1,128,256]{2,1,0:T(8,128)(2,1)S(1)}, u32[]{:S(2)}, u32[]{:S(2)}) collective-permute-start(bf16[1,128,256]{2,1,0:T(8,128)(2,1)S(1)} %get-tuple-element.27), channel_id=1, source_target_pairs={{1,0},{2,1},{3,2},{5,4},{6,5},{7,6},{9,8},{10,9},{11,10},{13,12},{... | collective-permute-start | bytes 196616 | tf_op jit(solution)/shard_map/ppermute | solution.py:15
  127.6 8.1 %collective-permute-start.2 = (bf16[1,128,256]{2,1,0:T(8,128)(2,1)S(1)}, bf16[1,128,256]{2,1,0:T(8,128)(2,1)S(1)}, u32[]{:S(2)}, u32[]{:S(2)}) collective-permute-start(bf16[1,128,256]{2,1,0:T(8,128)(2,1)S(1)} %get-tuple-element.28), channel_id=1, source_target_pairs={{0,1},{1,2},{2,3},{4,5},{5,6},{6,7},{8,9},{9,10},{10,11},{12,13},{... | collective-permute-start | bytes 196616 | tf_op jit(solution)/shard_map/ppermute | solution.py:14
  132.8 4.7 %collective-permute-start.1 = (bf16[1,128,256]{2,1,0:T(8,128)(2,1)S(1)}, bf16[1,128,256]{2,1,0:T(8,128)(2,1)S(1)}, u32[]{:S(2)}, u32[]{:S(2)}) collective-permute-start(bf16[1,128,256]{2,1,0:T(8,128)(2,1)S(1)} %get-tuple-element.29), channel_id=1, source_target_pairs={{4,0},{8,4},{12,8},{16,12},{20,16},{24,20},{28,24},{5,1},{9,5},{13... | collective-permute-start | bytes 196616 | tf_op jit(solution)/shard_map/ppermute | solution.py:15
Sparse Core Ops, SparseCore 0:
  60.3 130.3 all-reduce.2
where the time goes:
time: 202 us; the launch traced here: 201 us
  waiting for transfers between devices  54.3 us (27%)
  starting transfers between devices  44.1 us (22%)
  blocking collectives  40.9 us (20%)
  matrix products  22.9 us (11%)
  between operations  14.6 us (7%)
  other arithmetic  12.5 us (6%)
  local copies, waits for them, and re-layouts  11.8 us (6%)
    psum x1, waiting for transfers between devices, per_device(): lax.psum((grad_one, grad_two, grad_three), ('row', 'col'))  52.5 us
    psum x1, blocking collectives, per_device(): lax.psum((grad_one, grad_two, grad_three), ('row', 'col'))  40.9 us
    ppermute x8, starting transfers between devices, padded(): before = lax.ppermute(last, axis, up)  33.6 us
    ppermute x8, starting transfers between devices, padded(): after = lax.ppermute(initial, axis, down)  10.5 us
    dot_general x3, matrix products, spread(): summed = jnp.dot(local_bf, values, preferred_element_type=jnp.float32)  5.5 us
    unnamed x44, local copies, waits for them, and re-layouts  4.7 us
    reduce_sum x1, other arithmetic, per_device(): jnp.sum(local_mask, axis=1).astype(jnp.float32)  4.3 us
  transfers between devices with their start and end apart: 17, of which 2 were waited for; matrix products, arithmetic and copies ran while one was open for 10% of the time, Pallas kernels for 0%

commit v1 on v0

v1 whole, which is shorter than its diff:
```python
import functools

import jax
import jax.numpy as jnp
from jax import lax
from jax.experimental import pallas as pl
from jax.experimental.pallas import tpu as pltpu
from jax.sharding import PartitionSpec as P

MESH = pl.DeviceIdType.MESH
BF = jnp.bfloat16
F32 = jnp.float32


def up_to(value, step):
    return -(-value // step) * step


def dot(a, b, dims=((1,), (0,))):
    return lax.dot_general(a, b, (dims, ((), ())), preferred_element_type=F32)


def slope(pre):
    sigma = jax.nn.sigmoid(pre)
    return sigma * (1.0 + pre * (1.0 - sigma))


class Plan:
    def __init__(self, mesh, rows, width):
        self.n_row, self.n_col = mesh.shape["row"], mesh.shape["col"]
        self.pair = 2 if self.n_row % 2 == 0 else 1
        self.deep = self.n_row // self.pair
        self.offsets, at = [], 0
        for count in rows:
            self.offsets.append(at)
            at = up_to(at + count, 16)
        self.small = up_to(up_to(at, 16) // 16, self.n_row * self.n_col) * 16 // (self.n_row * self.n_col)
        self.quarter = self.small * self.deep
        self.half = self.quarter * self.n_col
        self.total = self.half * self.pair
        self.width = width

    def place(self):
        self.r, self.c = lax.axis_index("row"), lax.axis_index("col")
        self.core, self.z = self.r % self.pair, self.r // self.pair
        self.mate = self.r + 1 - 2 * self.core

    def col_peer(self, d):
        return (self.c + d) % self.n_col

    def deep_peer(self, d):
        return (self.z + d) % self.deep

    def deep_id(self, d):
        return (self.deep_peer(d) * self.pair + self.core, self.c)

    def greet(self):
        barrier = pltpu.get_barrier_semaphore()

        def hello(device):
            pl.semaphore_signal(barrier, inc=1, device_id=device, device_id_type=MESH)

        count = 0
        if self.pair == 2:
            hello((self.mate, self.c))
            count += 1
        for d in range(1, self.n_col):
            hello((self.r, self.col_peer(d)))
            count += 1
        for d in range(1, self.deep):
            hello(self.deep_id(d))
            count += 1
        for step, there in self.far_rows():
            @pl.when(there)
            def _():
                hello((self.r + step, self.c))
        for _, there in self.far_rows():
            count = count + jnp.where(there, 1, 0)
        pl.semaphore_wait(barrier, count)

    def far_rows(self):
        if self.pair == 2:
            return ((-1, jnp.logical_and(self.core == 0, self.r > 0)),
                    (1, jnp.logical_and(self.core == 1, self.r < self.n_row - 1)))
        return ()

    def edges(self):
        r, c = self.r, self.c
        return (((r - 1, c), 1, r > 0), ((r + 1, c), 0, r < self.n_row - 1),
                ((r, c - 1), 3, c > 0), ((r, c + 1), 2, c < self.n_col - 1))


def rows_at(start, count):
    return pl.ds(pl.multiple_of(start, 16), count)


def halo_copy(plan, k, src, dst, send, recv, way):
    bound = src.shape[0] // 4
    device, slot, there = plan.edges()[k]
    copy = pltpu.make_async_remote_copy(
        src_ref=src.at[pl.ds(k * bound, bound)], dst_ref=dst.at[pl.ds(slot * bound, bound)],
        send_sem=send.at[way, k], recv_sem=recv.at[way, slot], device_id=device, device_id_type=MESH)
    return copy, slot, there


def halo_start(plan, src, dst, send, recv, way):
    bound = src.shape[0] // 4
    for k in range(4):
        copy, _, there = halo_copy(plan, k, src, dst, send, recv, way)

        @pl.when(there)
        def _():
            copy.start()

        @pl.when(jnp.logical_not(there))
        def _():
            dst[pl.ds(k * bound, bound), :] = jnp.zeros((bound, dst.shape[1]), dst.dtype)


def halo_finish(plan, src, dst, send, recv, way):
    bound = src.shape[0] // 4
    for k in range(4):
        copy, _, there = halo_copy(plan, k, src, dst, send, recv, way)
        arrival = pltpu.make_async_remote_copy(
            src_ref=src.at[pl.ds(k * bound, bound)], dst_ref=dst.at[pl.ds(k * bound, bound)],
            send_sem=send.at[way, k], recv_sem=recv.at[way, k], device_id=plan.edges()[k][0], device_id_type=MESH)

        @pl.when(there)
        def _():
            copy.wait_send()
            arrival.wait_recv()


def reduce_all(plan, packed, packed_bf, got_pair, got_col, got_deep, acc_bf, whole, sems):
    pair_s, pair_r, col_s, col_r, deep_s, deep_r, gdeep_s, gdeep_r, gcol_s, gcol_r, gpair_s, gpair_r = sems
    half, quarter, small = plan.half, plan.quarter, plan.small

    def remote(src, dst, s, r, device):
        return pltpu.make_async_remote_copy(src_ref=src, dst_ref=dst, send_sem=s, recv_sem=r,
                                            device_id=device, device_id_type=MESH)

    mine = plan.core * half
    if plan.pair == 2:
        first = remote(packed_bf.at[rows_at((1 - plan.core) * half, half)], got_pair, pair_s, pair_r, (plan.mate, plan.c))
        first.start()
        first.wait()
        summed = packed[rows_at(mine, half), :] + got_pair[...].astype(F32)
    else:
        summed = packed[rows_at(mine, half), :]
    packed[rows_at(mine, half), :] = summed
    acc_bf[...] = summed.astype(BF)
    copies = []
    for d in range(1, plan.n_col):
        peer = plan.col_peer(d)
        copies.append(remote(acc_bf.at[rows_at(peer * quarter, quarter)], got_col.at[d - 1], col_s.at[d - 1], col_r.at[d - 1], (plan.r, peer)))
        copies[-1].start()
    own = mine + plan.c * quarter
    total = packed[rows_at(own, quarter), :]
    for d, copy in enumerate(copies):
        copy.wait()
        total = total + got_col[d].astype(F32)
    packed[rows_at(own, quarter), :] = total
    acc_bf[0:quarter, :] = total.astype(BF)
    copies = []
    for d in range(1, plan.deep):
        peer = plan.deep_peer(d)
        copies.append(remote(acc_bf.at[rows_at(peer * small, small)], got_deep.at[d - 1], deep_s.at[d - 1], deep_r.at[d - 1], plan.deep_id(d)))
        copies[-1].start()
    last = own + plan.z * small
    total = packed[rows_at(last, small), :]
    for d, copy in enumerate(copies):
        copy.wait()
        total = total + got_deep[d].astype(F32)
    whole[rows_at(last, small), :] = total.astype(BF)
    copies = []
    for d in range(1, plan.deep):
        part = whole.at[rows_at(last, small)]
        copies.append(remote(part, part, gdeep_s.at[d - 1], gdeep_r.at[d - 1], plan.deep_id(d)))
        copies[-1].start()
    for copy in copies:
        copy.wait()
    copies = []
    for d in range(1, plan.n_col):
        part = whole.at[rows_at(own, quarter)]
        copies.append(remote(part, part, gcol_s.at[d - 1], gcol_r.at[d - 1], (plan.r, plan.col_peer(d))))
        copies[-1].start()
    for copy in copies:
        copy.wait()
    if plan.pair == 2:
        part = whole.at[rows_at(mine, half)]
        final = remote(part, part, gpair_s, gpair_r, (plan.mate, plan.c))
        final.start()
        final.wait()


def traffic(plan, g1, g2, g3, s2, s3, o2, o3, out1, out2, out3, n2, n3, b2, b3,
            packed, packed_bf, got_pair, got_col, got_deep, acc_bf, whole, hsend, hrecv, *sems):
    plan.place()
    plan.greet()
    packed[...] = jnp.zeros_like(packed)
    for ref, at in zip((g1, g2, g3), plan.offsets):
        packed[at:at + ref.shape[0], :] = ref[...]
    packed_bf[...] = packed[...].astype(BF)
    trades = ((s2, n2), (s3, n3), (o3, b3), (o2, b2))
    for way, (src, dst) in enumerate(trades):
        halo_start(plan, src, dst, hsend, hrecv, way)
    reduce_all(plan, packed, packed_bf, got_pair, got_col, got_deep, acc_bf, whole, sems)
    for ref, at in zip((out1, out2, out3), plan.offsets):
        ref[...] = whole[at:at + ref.shape[0], :].astype(F32)
    for way, (src, dst) in enumerate(trades):
        halo_finish(plan, src, dst, hsend, hrecv, way)


def comm_scratch(plan):
    width = plan.width
    dma = pltpu.SemaphoreType.DMA
    peers, deep = max(plan.n_col - 1, 1), max(plan.deep - 1, 1)
    return [
        pltpu.VMEM((plan.total, width), F32), pltpu.VMEM((plan.total, width), BF),
        pltpu.VMEM((plan.half, width), BF), pltpu.VMEM((peers, plan.quarter, width), BF),
        pltpu.VMEM((deep, plan.small, width), BF), pltpu.VMEM((plan.half, width), BF),
        pltpu.VMEM((plan.total, width), BF), dma((4, 4)), dma((4, 4)),
        dma, dma, dma((peers,)), dma((peers,)), dma((deep,)), dma((deep,)),
        dma((deep,)), dma((deep,)), dma((peers,)), dma((peers,)), dma, dma]


def spread(local_bf, halo_bf, inverse, values, remote):
    summed = dot(local_bf, values) + values.astype(F32) + dot(halo_bf, remote)
    return (summed * inverse).astype(BF)


def retract(local_bf, halo_bf, inverse, upstream, weight, hits, returned):
    scaled = (dot(upstream, weight, ((1,), (1,))) * inverse).astype(BF)
    carried = dot(local_bf, scaled, ((0,), (0,))) + scaled.astype(F32) + dot(hits, returned)
    return carried, dot(halo_bf, scaled, ((0,), (0,))).astype(BF)


def per_device(mesh, features, local_mask, halo_mask, boundary_index, labels, halo_first, halo_second, halo_third,
               return_second, return_third, weight_first, weight_second, weight_third):
    features, local_mask, halo_mask = features[0, 0], local_mask[0, 0], halo_mask[0, 0]
    boundary_index, labels = boundary_index[0, 0], labels[0, 0]
    local_bf, halo_bf = local_mask.astype(BF), halo_mask.astype(BF)
    degree = 1.0 + jnp.sum(local_mask, axis=1).astype(F32) + jnp.sum(halo_mask, axis=1).astype(F32)
    inverse = (1.0 / degree)[:, None]
    nodes = features.shape[0]
    hits = (jnp.arange(nodes, dtype=jnp.int32)[:, None] == boundary_index[None, :]).astype(BF)
    mixed_one = spread(local_bf, halo_bf, inverse, features, halo_first[0, 0])
    pre_one = dot(mixed_one, weight_first)
    hidden_one = jax.nn.silu(pre_one).astype(BF)
    sent_second = dot(hits, hidden_one, ((0,), (0,))).astype(BF)
    mixed_two = spread(local_bf, halo_bf, inverse, hidden_one, halo_second[0, 0])
    pre_two = dot(mixed_two, weight_second)
    hidden_two = jax.nn.silu(pre_two).astype(BF)
    sent_third = dot(hits, hidden_two, ((0,), (0,))).astype(BF)
    mixed_three = spread(local_bf, halo_bf, inverse, hidden_two, halo_third[0, 0])
    logits = dot(mixed_three, weight_third)
    expo = jnp.exp(logits)
    probs = expo / jnp.sum(expo, axis=1, keepdims=True)
    target = (labels[:, None] == jnp.arange(logits.shape[1], dtype=jnp.int32)[None, :]).astype(F32)
    upstream_three = ((probs - target) / nodes).astype(BF)
    grad_three = dot(upstream_three, mixed_three, ((0,), (0,)))
    carried_two, outgoing_three = retract(local_bf, halo_bf, inverse, upstream_three, weight_third, hits, return_third[0, 0])
    upstream_two = (carried_two * slope(pre_two)).astype(BF)
    grad_two = dot(mixed_two, upstream_two, ((0,), (0,)))
    carried_one, outgoing_two = retract(local_bf, halo_bf, inverse, upstream_two, weight_second, hits, return_second[0, 0])
    upstream_one = (carried_one * slope(pre_one)).astype(BF)
    grad_one = dot(mixed_one, upstream_one, ((0,), (0,)))
    grads = (grad_one, grad_two, grad_three)
    plan = Plan(mesh, [g.shape[0] for g in grads], grad_one.shape[1])
    sent = (sent_second, sent_third, outgoing_two, outgoing_three)
    vmem = pl.BlockSpec(memory_space=pltpu.VMEM)
    done = pl.pallas_call(
        functools.partial(traffic, plan),
        out_shape=tuple(jax.ShapeDtypeStruct(v.shape, v.dtype) for v in grads + sent),
        in_specs=[vmem] * 7, out_specs=(vmem,) * 7, scratch_shapes=comm_scratch(plan),
        compiler_params=pltpu.CompilerParams(collective_id=0, has_side_effects=True),
        name="traffic",
    )(*grads, *sent)
    return (done[0], done[1], done[2].T) + tuple(v[None, None] for v in done[3:])


def solution(mesh):
    wide, flat, copied = P("row", "col", None, None), P("row", "col", None), P()
    return jax.shard_map(
        functools.partial(per_device, mesh), mesh=mesh,
        in_specs=(wide, wide, wide, flat, flat, wide, wide, wide, wide, wide, copied, copied, copied),
        out_specs=(copied, copied, copied, wide, wide, wide, wide),
        check_vma=False,
    )
```

time: 202 us -> 78.8 us (0.39)
  waiting for transfers between devices: 54.3 us -> 0 us
  starting transfers between devices: 44.1 us -> 0 us
  blocking collectives: 40.9 us -> 0 us
  Pallas kernels: 0 us -> 37.8 us
  between operations: 14.6 us -> 0.84 us
  other arithmetic: 12.5 us -> 6.99 us
    psum x1 -> x0, waiting for transfers between devices: 52.5 us -> none  [per_device(): lax.psum((grad_one, grad_two, grad_three), ('row', 'col'))]
    ppermute x16 -> x0, starting transfers between devices: 44.1 us -> none  [the longest x8 33.6 us: padded(): before = lax.ppermute(last, axis, up)]
    psum x1 -> x0, blocking collectives: 40.9 us -> none  [per_device(): lax.psum((grad_one, grad_two, grad_three), ('row', 'col'))]
    pallas_call x0 -> x1, Pallas kernels: none -> 37.8 us  [per_device(): pl.pallas_call(functools.partial(traffic, plan), out_shape=tuple((jax.Sha...]
    unnamed x44 -> x33, local copies, waits for them, and re-layouts: 4.7 us -> 10.1 us
    gather x2 -> x0, local copies, waits for them, and re-layouts: 3.89 us -> none  [the longest x1 1.95 us: per_device(): next_second = trade_features(jnp.take(hidden_one, boundary_index, axis=0))]
    concatenate x4 -> x0, other arithmetic: 3.33 us -> none  [arrange(): jnp.concatenate([vertical[0:1], vertical[3:4], lateral[0:1], lateral[3:4]...]
    dot_general x19 -> x21, matrix products: 22.9 us -> 22.5 us  [dot(): return lax.dot_general(a, b, (dims, ((), ())), preferred_element_type=F32)]
  transfers between devices with their start and end apart: 17 -> 0, of which waited for: 2 -> 0; matrix products, arithmetic and copies ran while one was open for 10% -> 0% of each run, Pallas kernels for 0% -> 0%
where the time goes in v1:
time: 78.8 us; the launch traced here: 78.3 us
  Pallas kernels  37.8 us (48%)
  matrix products  22.5 us (29%)
  local copies, waits for them, and re-layouts  10.1 us (13%)
  other arithmetic  6.99 us (9%)
  between operations  0.84 us (1%)
    pallas_call x1, Pallas kernels, per_device(): pl.pallas_call(functools.partial(traffic, plan), out_shape=tuple((jax.Sha...  37.8 us
    dot_general x21, matrix products, dot(): return lax.dot_general(a, b, (dims, ((), ())), preferred_element_type=F32)  22.5 us
    unnamed x33, local copies, waits for them, and re-layouts  10.1 us
    reduce_sum x1, other arithmetic, per_device(): jnp.sum(local_mask, axis=1).astype(F32)  4.3 us
    convert_element_type x1, other arithmetic, per_device(): local_bf, halo_bf = (local_mask.astype(BF), halo_mask.astype(BF))  2.68 us

profile of v1, /device:TPU:0, one launch (start us, length us, event | category | flops | bytes accessed | tf_op | source)
XLA Modules:
  0.0 78.3 jit_solution(158337008786818480)
XLA Ops:
  0.6 0.0 copy-start
  0.6 2.7 %fusion.80 = (bf16[1,1,1024,512]{3,2,1,0:T(8,128)(2,1)S(1)}, s32[1024]{0:T(1024)S(1)}) fusion(s32[1,1,1024,512]{3,2,1,0:T(8,128)} %param.15), kind=kLoop, calls=%fused_computation.78 | loop fusion | flops 1047552 | bytes 3149824 | tf_op jit(solution)/shard_map/convert_element_type | solution.py:242
  3.3 0.0 copy-start.1
  3.3 4.3 %fusion.79 = (s32[1024]{0:T(1024)S(1)}, bf16[1,1,1024,1024]{3,2,1,0:T(8,128)(2,1)S(1)}) fusion(s32[1,1,1024,1024]{3,2,1,0:T(8,128)} %param.14), kind=kLoop, calls=%fused_computation.77 | loop fusion | flops 2096128 | bytes 6295552 | tf_op jit(solution)/shard_map/reduce_sum | solution.py:243
  7.7 0.0 copy-done.1
  7.7 1.5 %fusion.8 = f32[1024,602]{0,1:T(8,128)S(1)} fusion(bf16[1,1,1024,1024]{3,2,1,0:T(8,128)(2,1)S(1)} %get-tuple-element.22, bf16[1,1,1024,602]{2,3,1,0:T(8,128)(2,1)S(1)} %copy-done.1), kind=kOutput, calls=%fused_computation.9 | convolution fusion | flops 1262485504 | bytes 5795840 | tf_op jit(solution)/shard_map/dot_general | solution.py:20
  9.2 0.0 copy-done
  9.2 0.0 copy-start.9
  9.2 0.9 %multiply_convert_fusion = bf16[1024,602]{0,1:T(8,128)(2,1)S(1)} fusion(f32[1024,602]{0,1:T(8,128)S(1)} %fusion.8, bf16[1,1,1024,602]{2,3,1,0:T(8,128)(2,1)S(1)} %copy-done.1, f32[1024]{0:T(1024)S(1)} %add_divide_fusion.3, bf16[1,1,1024,512]{3,2,1,0:T(8,128)(2,1)S(1)} %get-tuple-element.23, bf16[1,1,512,602]{2,3,1,0:T(8,128)(2,1)S(1)} %copy-done), kind=kOutput, calls=%fused_computation | convolution fusion | flops 634324992 | bytes 6600704 | tf_op jit(solution)/shard_map/dot_general | solution.py:20
  10.2 0.0 copy-done.9
  10.2 1.6 %multiply_convert_fusion.2 = (bf16[1024,256]{1,0:T(8,128)(2,1)S(1)}, f32[1024,256]{1,0:T(8,128)}) fusion(bf16[1024,602]{0,1:T(8,128)(2,1)S(1)} %multiply_convert_fusion, bf16[602,256]{1,0:T(8,128)(2,1)S(1)} %copy-done.9), kind=kOutput, calls=%fused_computation.64 | convolution fusion | flops 316932096 | bytes 3113984 | tf_op jit(solution)/shard_map/dot_general | solution.py:20
  11.8 0.0 copy-done.12
  11.8 1.5 %fusion.52.s2 = bf16[512,256]{1,0:T(8,128)(2,1)} fusion(bf16[1024,256]{1,0:T(8,128)(2,1)S(1)} %get-tuple-element.25, s32[512]{0:T(512)S(1)} %bitcast.113), kind=kOutput, calls=%fused_computation.42 | convolution fusion | flops 269090816 | bytes 788480 | tf_op jit(solution)/shard_map/dot_general | solution.py:20
  13.3 0.7 fusion.38
  14.0 0.2 copy-done.5
  14.2 0.4 fusion.45
  14.7 0.5 copy-done.7
  15.1 0.4 multiply_convert_fusion.1
  15.6 1.5 %fusion.53.s3 = bf16[512,256]{1,0:T(8,128)(2,1)} fusion(bf16[1024,256]{1,0:T(8,128)(2,1)S(1)} %get-tuple-element.27, s32[512]{0:T(512)S(1)} %bitcast.114), kind=kOutput, calls=%fused_computation.43 | convolution fusion | flops 269090816 | bytes 788480 | tf_op jit(solution)/shard_map/dot_general | solution.py:20
  17.1 0.7 fusion.41
  17.8 0.2 copy-done.6
  18.0 0.4 fusion.46
  18.5 0.3 copy-done.8
  18.7 0.3 fusion.81
  19.0 0.0 copy-done.11
  19.0 0.8 %fusion.78.g3 = f32[41,256]{1,0:T(8,128)} fusion(bf16[1024,256]{1,0:T(8,128)(2,1)S(1)} %fusion.46, f32[1024,41]{0,1:T(8,128)S(1)} %get-tuple-element.30, s32[1024]{0:T(1024)S(1)} %bitcast.111, f32[1024]{0:T(1024)S(1)} %get-tuple-element.29), kind=kOutput, calls=%fused_computation.76 | convolution fusion | flops 21747712 | bytes 742400 | tf_op jit(solution)/shard_map/dot_general | solution.py:20
  19.9 0.4 fusion.44
  20.2 1.2 %fusion.55.o3 = bf16[512,256]{1,0:T(8,128)(2,1)} fusion(bf16[1024,256]{1,0:T(8,128)(2,1)S(1)} %fusion.44, bf16[1,1,1024,512]{3,2,1,0:T(8,128)(2,1)S(1)} %get-tuple-element.23), kind=kOutput, calls=%fused_computation.47 | convolution fusion | flops 268566528 | bytes 1835008 | tf_op jit(solution)/shard_map/dot_general | solution.py:20
  21.5 1.0 %fusion.35 = f32[1024,256]{1,0:T(8,128)S(1)} fusion(bf16[1024,256]{1,0:T(8,128)(2,1)S(1)} %fusion.44, bf16[1,1,1024,1024]{3,2,1,0:T(8,128)(2,1)S(1)} %get-tuple-element.22), kind=kOutput, calls=%fused_computation.31 | convolution fusion | flops 537395200 | bytes 3670016 | tf_op jit(solution)/shard_map/dot_general | solution.py:20
  22.4 0.0 copy-done.10
  22.4 0.8 fusion.48
  23.2 1.0 %fusion.82.g2 = f32[256,256]{1,0:T(8,128)} fusion(bf16[1024,256]{1,0:T(8,128)(2,1)S(1)} %fusion.45, bf16[1024,256]{1,0:T(8,128)(2,1)S(1)} %fusion.48), kind=kOutput, calls=%fused_computation.80 | convolution fusion | flops 134217728 | bytes 1310720 | tf_op jit(solution)/shard_map/dot_general | solution.py:20
  24.3 0.3 fusion.49
  24.6 2.0 %fusion.32 = f32[1024,256]{1,0:T(8,128)} fusion(bf16[1024,256]{1,0:T(8,128)(2,1)S(1)} %fusion.49, bf16[1,1,1024,1024]{3,2,1,0:T(8,128)(2,1)S(1)} %get-tuple-element.22), kind=kOutput, calls=%fused_computation.30 | convolution fusion | flops 537395200 | bytes 3670016 | tf_op jit(solution)/shard_map/dot_general | solution.py:20
  26.6 3.7 %fusion.51.g1 = f32[602,256]{1,0:T(8,128)} fusion(bf16[1024,602]{0,1:T(8,128)(2,1)S(1)} %multiply_convert_fusion, f32[1024,256]{1,0:T(8,128)} %fusion.32, f32[1024,256]{1,0:T(8,128)} %get-tuple-element.26, s32[512]{0:T(512)S(1)} %bitcast.116, bf16[1,1,512,256]{3,2,1,0:T(8,128)(2,1)} %param.21), kind=kOutput, calls=%fused_computation.41 | convolution fusion | flops 587202560 | bytes 4210688 | tf_op jit(solution)/shard_map/dot_general | solution.py:20
  30.3 1.2 %fusion.54.o2 = bf16[512,256]{1,0:T(8,128)(2,1)} fusion(bf16[1024,256]{1,0:T(8,128)(2,1)S(1)} %fusion.49, bf16[1,1,1024,512]{3,2,1,0:T(8,128)(2,1)S(1)} %get-tuple-element.23), kind=kOutput, calls=%fused_computation.46 | convolution fusion | flops 268566528 | bytes 1835008 | tf_op jit(solution)/shard_map/dot_general | solution.py:20
  31.5 37.8 %traffic.1 = (f32[602,256]{1,0:T(8,128)}, f32[256,256]{1,0:T(8,128)}, f32[41,256]{1,0:T(8,128)}, bf16[512,256]{1,0:T(8,128)(2,1)}, bf16[512,256]{1,0:T(8,128)(2,...) custom-call(f32[602,256]{1,0:T(8,128)} %fusion.51.g1, f32[256,256]{1,0:T(8,128)} %fusion.82.g2, ...), custom_call_target="tpu_custom_call" | custom-call | tf_op jit(solution)/shard_map/traffic/pallas_call | solution.py:272
  69.4 0.0 copy-start.4
  69.4 0.0 copy-start.3
  69.4 0.0 copy-start.2
  69.4 2.0 %copy.37 = f32[602,256]{1,0:T(8,128)} copy(f32[602,256]{1,0:T(8,128)} %get-tuple-element.38) | data formatting | bytes 1232896
  71.4 1.7 %copy.38 = f32[256,256]{1,0:T(8,128)} copy(f32[256,256]{1,0:T(8,128)} %get-tuple-element.39) | data formatting | bytes 524288
  73.1 1.4 %copy.39 = f32[256,41]{0,1:T(8,128)} copy(f32[256,41]{0,1:T(8,128)} %bitcast.110) | data formatting | bytes 83968
  74.5 1.7 %copy.40 = bf16[1,1,512,256]{3,2,1,0:T(8,128)(2,1)} copy(bf16[1,1,512,256]{3,2,1,0:T(8,128)(2,1)} %bitcast.109) | data formatting | bytes 524288
  76.2 0.0 copy-done.4
  76.2 0.7 copy.41
  76.9 0.7 copy.42
  77.6 0.7 copy.43
  (10 shorter events, 0.0 us)
Async XLA Ops:
  0.6 8.6 %copy-start = (bf16[1,1,512,602]{2,3,1,0:T(8,128)(2,1)S(1)}, bf16[1,1,512,602]{2,3,1,0:T(8,128)(2,1)}, u32[]{:S(2)}) copy-start(bf16[1,1,512,602]{2,3,1,0:T(8,128)(2,1)} %param.18) | copy-start | bytes 1849348
  3.3 4.3 %copy-start.1 = (bf16[1,1,1024,602]{2,3,1,0:T(8,128)(2,1)S(1)}, bf16[1,1,1024,602]{2,3,1,0:T(8,128)(2,1)}, u32[]{:S(2)}) copy-start(bf16[1,1,1024,602]{2,3,1,0:T(8,128)(2,1)} %param.13) | copy-start | bytes 3698692
  9.2 1.0 %copy-start.9 = (bf16[602,256]{1,0:T(8,128)(2,1)S(1)}, bf16[602,256]{1,0:T(8,128)(2,1)}, u32[]{:S(2)}) copy-start(bf16[602,256]{1,0:T(8,128)(2,1)} %param.23) | copy-start | bytes 924676
  10.2 1.6 %copy-start.12 = (s32[1,1,512]{2,1,0:T(1,128)S(1)}, s32[1,1,512]{2,1,0:T(1,128)}, u32[]{:S(2)}) copy-start(s32[1,1,512]{2,1,0:T(1,128)} %param.16) | copy-start | bytes 6148
  13.3 0.9 %copy-start.5 = (bf16[1,1,512,256]{3,2,1,0:T(8,128)(2,1)S(1)}, bf16[1,1,512,256]{3,2,1,0:T(8,128)(2,1)}, u32[]{:S(2)}) copy-start(bf16[1,1,512,256]{3,2,1,0:T(8,128)(2,1)} %param.19) | copy-start | bytes 786436
  14.2 0.9 %copy-start.7 = (bf16[256,256]{1,0:T(8,128)(2,1)S(1)}, bf16[256,256]{1,0:T(8,128)(2,1)}, u32[]{:S(2)}) copy-start(bf16[256,256]{1,0:T(8,128)(2,1)} %param.24) | copy-start | bytes 393220
  17.1 0.9 %copy-start.6 = (bf16[1,1,512,256]{3,2,1,0:T(8,128)(2,1)S(1)}, bf16[1,1,512,256]{3,2,1,0:T(8,128)(2,1)}, u32[]{:S(2)}) copy-start(bf16[1,1,512,256]{3,2,1,0:T(8,128)(2,1)} %param.20) | copy-start | bytes 786436
  18.0 0.7 copy-start.8
  18.0 1.0 %copy-start.11 = (s32[1,1,1024]{2,1,0:T(1,128)S(1)}, s32[1,1,1024]{2,1,0:T(1,128)}, u32[]{:S(2)}) copy-start(s32[1,1,1024]{2,1,0:T(1,128)} %param.17) | copy-start | bytes 12292
  21.5 1.0 %copy-start.10 = (bf16[1,1,512,256]{3,2,1,0:T(8,128)(2,1)S(1)}, bf16[1,1,512,256]{3,2,1,0:T(8,128)(2,1)}, u32[]{:S(2)}) copy-start(bf16[1,1,512,256]{3,2,1,0:T(8,128)(2,1)} %param.22) | copy-start | bytes 786436
  69.4 6.8 %copy-start.4 = (bf16[512,256]{1,0:T(8,128)(2,1)S(1)}, bf16[512,256]{1,0:T(8,128)(2,1)}, u32[]{:S(2)}) copy-start(bf16[512,256]{1,0:T(8,128)(2,1)} %get-tuple-element.18) | copy-start | bytes 786436
  69.4 7.5 %copy-start.3 = (bf16[512,256]{1,0:T(8,128)(2,1)S(1)}, bf16[512,256]{1,0:T(8,128)(2,1)}, u32[]{:S(2)}) copy-start(bf16[512,256]{1,0:T(8,128)(2,1)} %get-tuple-element.19) | copy-start | bytes 786436
  69.4 8.2 %copy-start.2 = (bf16[512,256]{1,0:T(8,128)(2,1)S(1)}, bf16[512,256]{1,0:T(8,128)(2,1)}, u32[]{:S(2)}) copy-start(bf16[512,256]{1,0:T(8,128)(2,1)} %get-tuple-element.20) | copy-start | bytes 786436

commit v2 on v1

v2 whole, which is shorter than its diff:
```python
import functools

import jax
import jax.numpy as jnp
from jax import lax
from jax.experimental import pallas as pl
from jax.experimental.pallas import tpu as pltpu
from jax.sharding import PartitionSpec as P

MESH = pl.DeviceIdType.MESH
BF = jnp.bfloat16
F32 = jnp.float32


def up_to(value, step):
    return -(-value // step) * step


def dot(a, b, dims=((1,), (0,))):
    return lax.dot_general(a, b, (dims, ((), ())), preferred_element_type=F32)


def slope(pre):
    sigma = jax.nn.sigmoid(pre)
    return sigma * (1.0 + pre * (1.0 - sigma))


class Plan:
    def __init__(self, mesh, first, second, third):
        self.n_row, self.n_col = mesh.shape["row"], mesh.shape["col"]
        self.pair = 2 if self.n_row % 2 == 0 else 1
        self.deep = self.n_row // self.pair
        self.small = 16
        self.quarter = self.small * self.deep
        self.half = self.quarter * self.n_col
        self.piece = self.half * self.pair
        self.lanes = 128 if first[1] % 128 == 0 else first[1]
        self.strips = first[1] // self.lanes
        self.at_second = 0
        self.early = up_to(up_to(second[0], 16) * self.strips, self.piece) // self.piece
        self.at_first = self.early * self.piece
        self.at_third = self.at_first + up_to(first[0], 16) * self.strips
        self.pieces = up_to(self.at_third + up_to(third[0], 16) * self.strips, self.piece) // self.piece
        self.total = self.pieces * self.piece

    def strip(self, at, count, j):
        at = at + j * up_to(count, 16)
        return slice(at, at + count), slice(j * self.lanes, (j + 1) * self.lanes)

    def place(self):
        self.r, self.c = lax.axis_index("row"), lax.axis_index("col")
        self.core, self.z = self.r % self.pair, self.r // self.pair
        self.mate = self.r + 1 - 2 * self.core

    def col_peer(self, d):
        return (self.c + d) % self.n_col

    def deep_peer(self, d):
        return (self.z + d) % self.deep

    def deep_id(self, d):
        return (self.deep_peer(d) * self.pair + self.core, self.c)

    def greet(self):
        barrier = pltpu.get_barrier_semaphore()

        def hello(device):
            pl.semaphore_signal(barrier, inc=1, device_id=device, device_id_type=MESH)

        count = 0
        if self.pair == 2:
            hello((self.mate, self.c))
            count += 1
        for d in range(1, self.n_col):
            hello((self.r, self.col_peer(d)))
            count += 1
        for d in range(1, self.deep):
            hello(self.deep_id(d))
            count += 1
        for step, there in self.far_rows():
            @pl.when(there)
            def _():
                hello((self.r + step, self.c))
        for _, there in self.far_rows():
            count = count + jnp.where(there, 1, 0)
        pl.semaphore_wait(barrier, count)

    def far_rows(self):
        if self.pair == 2:
            return ((-1, jnp.logical_and(self.core == 0, self.r > 0)),
                    (1, jnp.logical_and(self.core == 1, self.r < self.n_row - 1)))
        return ()

    def edges(self):
        r, c = self.r, self.c
        return (((r - 1, c), 1, r > 0), ((r + 1, c), 0, r < self.n_row - 1),
                ((r, c - 1), 3, c > 0), ((r, c + 1), 2, c < self.n_col - 1))


def rows_at(start, count):
    return pl.ds(pl.multiple_of(start, 16), count)


def halo_copy(plan, k, src, dst, send, recv, way):
    bound = src.shape[0] // 4
    device, slot, there = plan.edges()[k]
    copy = pltpu.make_async_remote_copy(
        src_ref=src.at[pl.ds(k * bound, bound)], dst_ref=dst.at[pl.ds(slot * bound, bound)],
        send_sem=send.at[way, k], recv_sem=recv.at[way, slot], device_id=device, device_id_type=MESH)
    return copy, slot, there


def halo_start(plan, src, dst, send, recv, way):
    bound = src.shape[0] // 4
    for k in range(4):
        copy, _, there = halo_copy(plan, k, src, dst, send, recv, way)

        @pl.when(there)
        def _():
            copy.start()

        @pl.when(jnp.logical_not(there))
        def _():
            dst[pl.ds(k * bound, bound), :] = jnp.zeros((bound, dst.shape[1]), dst.dtype)


def halo_finish(plan, src, dst, send, recv, way):
    bound = src.shape[0] // 4
    for k in range(4):
        copy, _, there = halo_copy(plan, k, src, dst, send, recv, way)
        arrival = pltpu.make_async_remote_copy(
            src_ref=src.at[pl.ds(k * bound, bound)], dst_ref=dst.at[pl.ds(k * bound, bound)],
            send_sem=send.at[way, k], recv_sem=recv.at[way, k], device_id=plan.edges()[k][0], device_id_type=MESH)

        @pl.when(there)
        def _():
            copy.wait_send()
            arrival.wait_recv()


class Summer:
    STAGES = 6

    def __init__(self, plan, packed, packed_bf, got_pair, got_col, got_deep, acc_bf, whole, sems):
        self.plan, self.packed, self.packed_bf, self.whole = plan, packed, packed_bf, whole
        self.got_pair, self.got_col, self.got_deep, self.acc_bf = got_pair, got_col, got_deep, acc_bf
        self.sems = sems
        self.flying = {}
        self.stage = [0] * plan.pieces

    def copy(self, p, src, dst, kind, d, device):
        copy = pltpu.make_async_remote_copy(
            src_ref=src, dst_ref=dst, send_sem=self.sems[2 * kind].at[p, d], recv_sem=self.sems[2 * kind + 1].at[p, d],
            device_id=device, device_id_type=MESH)
        copy.start()
        self.flying[p].append(copy)

    def land(self, p):
        for copy in self.flying.get(p, ()):
            copy.wait()
        self.flying[p] = []

    def advance(self, p):
        plan, base = self.plan, p * self.plan.piece
        half, quarter, small = plan.half, plan.quarter, plan.small
        mine = base + plan.core * half
        own = mine + plan.c * quarter
        last = own + plan.z * small
        packed, whole, acc = self.packed, self.whole, self.acc_bf.at[p]
        stage = self.stage[p]
        self.stage[p] += 1
        self.land(p)
        if stage == 0 and plan.pair == 2:
            self.copy(p, self.packed_bf.at[rows_at(base + (1 - plan.core) * half, half)], self.got_pair.at[p], 0, 0, (plan.mate, plan.c))
        elif stage == 1:
            total = packed[rows_at(mine, half), :]
            if plan.pair == 2:
                total = total + self.got_pair[p].astype(F32)
            packed[rows_at(mine, half), :] = total
            acc[...] = total.astype(BF)
            for d in range(1, plan.n_col):
                peer = plan.col_peer(d)
                self.copy(p, acc.at[rows_at(peer * quarter, quarter)], self.got_col.at[p, d - 1], 1, d - 1, (plan.r, peer))
        elif stage == 2:
            total = packed[rows_at(own, quarter), :]
            for d in range(1, plan.n_col):
                total = total + self.got_col[p, d - 1].astype(F32)
            packed[rows_at(own, quarter), :] = total
            acc[0:quarter, :] = total.astype(BF)
            for d in range(1, plan.deep):
                self.copy(p, acc.at[rows_at(plan.deep_peer(d) * small, small)], self.got_deep.at[p, d - 1], 2, d - 1, plan.deep_id(d))
        elif stage == 3:
            total = packed[rows_at(last, small), :]
            for d in range(1, plan.deep):
                total = total + self.got_deep[p, d - 1].astype(F32)
            whole[rows_at(last, small), :] = total.astype(BF)
            part = whole.at[rows_at(last, small)]
            for d in range(1, plan.deep):
                self.copy(p, part, part, 3, d - 1, plan.deep_id(d))
        elif stage == 4:
            part = whole.at[rows_at(own, quarter)]
            for d in range(1, plan.n_col):
                self.copy(p, part, part, 4, d - 1, (plan.r, plan.col_peer(d)))
        elif stage == 5 and plan.pair == 2:
            part = whole.at[rows_at(mine, half)]
            self.copy(p, part, part, 5, 0, (plan.mate, plan.c))


NAMES = ("local", "halo", "features", "halo_first", "halo_second", "halo_third", "return_second", "return_third",
         "weight_first", "weight_second", "weight_third", "index_row", "index_col", "labels")


def step_kernel(plan, tiles, *refs):
    count = len(NAMES)
    hbm = dict(zip(NAMES, refs[:count]))
    whole, n2, n3, b2, b3 = refs[count:count + 5]
    held = dict(zip(NAMES, refs[count + 5:2 * count + 5]))
    (in_sem, local_bf, halo_bf, inverse, hits, hits_t, mixed_one, mixed_two, mixed_three, pre_one, pre_two, hidden_one,
     hidden_two, scaled, upstream, upstream_three, s2, s3, o2, o3, hsend, hrecv,
     packed, packed_bf, got_pair, got_col, got_deep, acc_bf) = refs[2 * count + 5:2 * count + 33]
    sems = refs[2 * count + 33:]
    nodes = held["features"].shape[0]
    tall = nodes // tiles
    tile = [pl.ds(t * tall, tall) for t in range(tiles)]
    plan.place()

    loads = {}
    for name in ("index_row", "index_col", "features", "halo_first", "local", "halo") + NAMES[4:11] + ("labels",):
        if name in ("local", "halo"):
            for t in range(tiles):
                key = (name, t)
                loads[key] = pltpu.make_async_copy(hbm[name].at[tile[t]], held[name].at[tile[t]], in_sem.at[len(loads)])
        else:
            loads[name] = pltpu.make_async_copy(hbm[name], held[name], in_sem.at[len(loads)])
    order = ["index_row", "index_col", "features", "halo_first"]
    for t in range(tiles):
        order += [("local", t), ("halo", t)]
    order += [name for name in loads if name not in order]
    for key in order:
        loads[key].start()

    plan.greet()
    packed[...] = jnp.zeros_like(packed)
    packed_bf[...] = jnp.zeros_like(packed_bf)
    summer = Summer(plan, packed, packed_bf, got_pair, got_col, got_deep, acc_bf, whole, sems)

    def put(value, at):
        for j in range(plan.strips):
            rows, lanes = plan.strip(at, value.shape[0], j)
            packed[rows, :] = value[:, lanes]
            packed_bf[rows, :] = value[:, lanes].astype(BF)

    loads["index_row"].wait()
    loads["index_col"].wait()
    slots = hits.shape[1]
    hits[...] = jnp.where(lax.broadcasted_iota(jnp.int32, (nodes, slots), 0) == held["index_row"][...], 1.0, 0.0).astype(BF)
    hits_t[...] = jnp.where(lax.broadcasted_iota(jnp.int32, (slots, nodes), 1) == held["index_col"][...], 1.0, 0.0).astype(BF)
    loads["features"].wait()
    loads["halo_first"].wait()

    def spread(t, values, remote, out):
        total = dot(local_bf[tile[t], :], values[...]) + values[tile[t], :].astype(F32) + dot(halo_bf[tile[t], :], remote[...])
        out[tile[t], :] = (total * inverse[tile[t], :]).astype(BF)

    for t in range(tiles):
        loads[("local", t)].wait()
        loads[("halo", t)].wait()
        near, far = held["local"][tile[t], :].astype(F32), held["halo"][tile[t], :].astype(F32)
        local_bf[tile[t], :] = near.astype(BF)
        halo_bf[tile[t], :] = far.astype(BF)
        inverse[tile[t], :] = 1.0 / (1.0 + jnp.sum(near, axis=1, keepdims=True) + jnp.sum(far, axis=1, keepdims=True))
        spread(t, held["features"], held["halo_first"], mixed_one)
        if t == 0:
            for name in NAMES[4:11] + ("labels",):
                loads[name].wait()
        pre = dot(mixed_one[tile[t], :], held["weight_first"][...])
        pre_one[tile[t], :] = pre
        hidden_one[tile[t], :] = (pre * jax.nn.sigmoid(pre)).astype(BF)
    s2[...] = dot(hits_t[...], hidden_one[...]).astype(BF)
    halo_start(plan, s2, n2, hsend, hrecv, 0)
    for t in range(tiles):
        spread(t, hidden_one, held["halo_second"], mixed_two)
        pre = dot(mixed_two[tile[t], :], held["weight_second"][...])
        pre_two[tile[t], :] = pre
        hidden_two[tile[t], :] = (pre * jax.nn.sigmoid(pre)).astype(BF)
    s3[...] = dot(hits_t[...], hidden_two[...]).astype(BF)
    halo_start(plan, s3, n3, hsend, hrecv, 1)
    for t in range(tiles):
        spread(t, hidden_two, held["halo_third"], mixed_three)
        logits = dot(mixed_three[tile[t], :], held["weight_third"][...])
        expo = jnp.exp(logits)
        probs = expo / jnp.sum(expo, axis=1, keepdims=True)
        target = jnp.where(held["labels"][tile[t], :] == lax.broadcasted_iota(jnp.int32, logits.shape, 1), 1.0, 0.0)
        up = ((probs - target) / nodes).astype(BF)
        upstream_three[tile[t], :] = up
        scaled[tile[t], :] = (dot(up, held["weight_third"][...], ((1,), (1,))) * inverse[tile[t], :]).astype(BF)
    turn = ((0,), (0,))

    def carry(t, returned):
        return dot(local_bf[:, tile[t]], scaled[...], turn) + scaled[tile[t], :].astype(F32) + dot(hits[tile[t], :], returned[...])

    for t in range(tiles):
        upstream[tile[t], :] = (carry(t, held["return_third"]) * slope(pre_two[tile[t], :])).astype(BF)
    put(dot(mixed_two[...], upstream[...], turn), plan.at_second)
    for p in range(plan.early):
        summer.advance(p)
    o3[...] = dot(halo_bf[...], scaled[...], turn).astype(BF)
    halo_start(plan, o3, b3, hsend, hrecv, 2)
    put(dot(upstream_three[...], mixed_three[...], turn), plan.at_third)
    for t in range(tiles):
        across = dot(upstream[tile[t], :], held["weight_second"][...], ((1,), (1,)))
        scaled[tile[t], :] = (across * inverse[tile[t], :]).astype(BF)
    for p in range(plan.early):
        summer.advance(p)
    for t in range(tiles):
        upstream[tile[t], :] = (carry(t, held["return_second"]) * slope(pre_one[tile[t], :])).astype(BF)
    for p in range(plan.early):
        summer.advance(p)
    put(dot(mixed_one[...], upstream[...], turn), plan.at_first)
    for p in range(plan.early, plan.pieces):
        summer.advance(p)
    for p in range(plan.early):
        summer.advance(p)
    o2[...] = dot(halo_bf[...], scaled[...], turn).astype(BF)
    halo_start(plan, o2, b2, hsend, hrecv, 3)
    for stage in range(1, Summer.STAGES):
        for p in list(range(plan.early, plan.pieces)) + list(range(plan.early)):
            if summer.stage[p] < Summer.STAGES:
                summer.advance(p)
    for p in range(plan.pieces):
        summer.land(p)
    for way, (src, dst) in enumerate(((s2, n2), (s3, n3), (o3, b3), (o2, b2))):
        halo_finish(plan, src, dst, hsend, hrecv, way)


def finish_kernel(plan, whole, n2, n3, b2, b3, g1, g2, g3, m2, m3, a2, a3, h1, h2, h3, sem):
    copies = [pltpu.make_async_copy(src, dst, sem.at[i]) for i, (src, dst) in enumerate(((n2, m2), (n3, m3), (b2, a2), (b3, a3)))]
    for copy in copies:
        copy.start()
    for ref, at in ((h1, plan.at_first), (h2, plan.at_second)):
        for j in range(plan.strips):
            rows, lanes = plan.strip(at, ref.shape[0], j)
            ref[:, lanes] = whole[rows, :].astype(F32)
    classes = h3.shape[1]
    for j in range(plan.strips):
        rows, lanes = plan.strip(plan.at_third, up_to(classes, 16), j)
        h3[lanes, :] = whole[rows, :].astype(F32).T[:, :classes]
    for i, (src, dst) in enumerate(((h1, g1), (h2, g2), (h3, g3))):
        copies.append(pltpu.make_async_copy(src, dst, sem.at[4 + i]))
        copies[-1].start()
    for copy in copies:
        copy.wait()


def per_device(mesh, features, local_mask, halo_mask, boundary_index, labels, halo_first, halo_second, halo_third,
               return_second, return_third, weight_first, weight_second, weight_third):
    features, local_mask, halo_mask = features[0, 0], local_mask[0, 0], halo_mask[0, 0]
    index, labels = boundary_index[0, 0], labels[0, 0]
    halo_first, halo_second, halo_third = halo_first[0, 0], halo_second[0, 0], halo_third[0, 0]
    return_second, return_third = return_second[0, 0], return_third[0, 0]
    nodes, width = features.shape
    slots, hidden, classes = index.shape[0], weight_first.shape[1], weight_third.shape[1]
    plan = Plan(mesh, weight_first.shape, weight_second.shape, weight_third.shape[::-1])
    tiles = 4 if nodes % 512 == 0 else 1
    values = (local_mask, halo_mask, features, halo_first, halo_second, halo_third, return_second, return_third,
              weight_first, weight_second, weight_third, index[None, :], index[:, None], labels[:, None])
    vmem, anywhere = pl.BlockSpec(memory_space=pltpu.VMEM), pl.BlockSpec(memory_space=pl.ANY)
    dma = pltpu.SemaphoreType.DMA
    peers, deep, n, lanes = max(plan.n_col - 1, 1), max(plan.deep - 1, 1), plan.pieces, plan.lanes
    block = jax.ShapeDtypeStruct((slots, hidden), BF)
    done = pl.pallas_call(
        functools.partial(step_kernel, plan, tiles),
        out_shape=(jax.ShapeDtypeStruct((plan.total, lanes), BF),) + (block,) * 4,
        in_specs=[anywhere] * len(values), out_specs=(vmem,) * 5,
        scratch_shapes=[pltpu.VMEM(v.shape, v.dtype) for v in values] + [
            dma((len(values) + 2 * tiles,)), pltpu.VMEM((nodes, nodes), BF), pltpu.VMEM((nodes, slots), BF), pltpu.VMEM((nodes, 1), F32),
            pltpu.VMEM((nodes, slots), BF), pltpu.VMEM((slots, nodes), BF),
            pltpu.VMEM((nodes, width), BF), pltpu.VMEM((nodes, hidden), BF), pltpu.VMEM((nodes, hidden), BF),
            pltpu.VMEM((nodes, hidden), F32), pltpu.VMEM((nodes, hidden), F32),
            pltpu.VMEM((nodes, hidden), BF), pltpu.VMEM((nodes, hidden), BF), pltpu.VMEM((nodes, hidden), BF),
            pltpu.VMEM((nodes, hidden), BF), pltpu.VMEM((nodes, classes), BF)]
        + [pltpu.VMEM((slots, hidden), BF)] * 4 + [dma((4, 4)), dma((4, 4)),
            pltpu.VMEM((plan.total, lanes), F32), pltpu.VMEM((plan.total, lanes), BF),
            pltpu.VMEM((n, plan.half, lanes), BF), pltpu.VMEM((n, peers, plan.quarter, lanes), BF),
            pltpu.VMEM((n, deep, plan.small, lanes), BF), pltpu.VMEM((n, plan.half, lanes), BF),
            dma((n, 1)), dma((n, 1)), dma((n, peers)), dma((n, peers)), dma((n, deep)), dma((n, deep)),
            dma((n, deep)), dma((n, deep)), dma((n, peers)), dma((n, peers)), dma((n, 1)), dma((n, 1))],
        compiler_params=pltpu.CompilerParams(collective_id=0, has_side_effects=True),
        name="step",
    )(*values)
    whole, n2, n3, b2, b3 = done
    grads = ((weight_first.shape, F32), (weight_second.shape, F32), (weight_third.shape, F32))
    out = pl.pallas_call(
        functools.partial(finish_kernel, plan),
        out_shape=tuple(jax.ShapeDtypeStruct(*g) for g in grads) + (block,) * 4,
        in_specs=[vmem] * 5, out_specs=(anywhere,) * 7,
        scratch_shapes=[pltpu.VMEM(*g) for g in grads] + [dma((7,))],
        name="finish",
    )(whole, n2, n3, b2, b3)
    return out[:3] + tuple(v[None, None] for v in out[3:])


def solution(mesh):
    wide, flat, copied = P("row", "col", None, None), P("row", "col", None), P()
    return jax.shard_map(
        functools.partial(per_device, mesh), mesh=mesh,
        in_specs=(wide, wide, wide, flat, flat, wide, wide, wide, wide, wide, copied, copied, copied),
        out_specs=(copied, copied, copied, wide, wide, wide, wide),
        check_vma=False,
    )
```

time: 78.8 us -> 62.3 us (0.79)
  matrix products: 22.5 us -> 0 us
  Pallas kernels: 37.8 us -> 51.3 us
  other arithmetic: 6.99 us -> 0 us
    dot_general x21 -> x0, matrix products: 22.5 us -> none  [dot(): return lax.dot_general(a, b, (dims, ((), ())), preferred_element_type=F32)]
    pallas_call x1 -> x2, Pallas kernels: 37.8 us -> 51.3 us  [the longest x1 48.6 us: per_device(): pl.pallas_call(functools.partial(step_kernel, plan, tiles), out_shape=(ja...]
    reduce_sum x1 -> x0, other arithmetic: 4.3 us -> none  [per_device(): jnp.sum(local_mask, axis=1).astype(F32)]
    unnamed x33 -> x6, local copies, waits for them, and re-layouts: 10.1 us -> 6.84 us
    another operation x0 -> x2, local copies, waits for them, and re-layouts: none -> 3.24 us  [the longest x1 1.71 us: per_device(): labels[:, None]]
    convert_element_type x1 -> x0, other arithmetic: 2.68 us -> none  [per_device(): local_bf, halo_bf = (local_mask.astype(BF), halo_mask.astype(BF))]
where the time goes in v2:
time: 62.3 us; the launch traced here: 62 us
  Pallas kernels  51.3 us (82%)
  local copies, waits for them, and re-layouts  10.1 us (16%)
  between operations  0.66 us (1%)
    pallas_call x1, Pallas kernels, per_device(): pl.pallas_call(functools.partial(step_kernel, plan, tiles), out_shape=(ja...  48.6 us
    unnamed x6, local copies, waits for them, and re-layouts  6.84 us
    pallas_call x1, Pallas kernels, per_device(): pl.pallas_call(functools.partial(finish_kernel, plan), out_shape=tuple((j...  2.69 us
    another operation x1, local copies, waits for them, and re-layouts, per_device(): labels[:, None]  1.71 us
    another operation x1, local copies, waits for them, and re-layouts, per_device(): index[:, None]  1.53 us

profile of v2, /device:TPU:0, one launch (start us, length us, event | category | flops | bytes accessed | tf_op | source)
XLA Modules:
  0.0 62.0 jit_solution(15557494862505542887)
XLA Ops:
  0.6 0.0 copy-start
  0.6 1.6 %copy.26.refs_10_ = bf16[256,41]{1,0:T(8,128)(2,1)} copy(bf16[256,41]{0,1:T(8,128)(2,1)} %param.25) | data formatting | bytes 41984 | tf_op args[12]
  2.2 1.5 %copy.27.refs_12_ = s32[512,1]{1,0:T(8,128)} copy(s32[512,1]{0,1:T(1,128)} %bitcast.23) | data formatting | bytes 4096 | tf_op jit(solution)/shard_map/broadcast_in_dim;squeeze | solution.py:366
  3.8 1.7 %copy.28.refs_13_ = s32[1024,1]{1,0:T(8,128)} copy(s32[1024,1]{0,1:T(1,128)} %bitcast.25) | data formatting | bytes 8192 | tf_op jit(solution)/shard_map/broadcast_in_dim;squeeze | solution.py:366
  5.5 2.2 %copy.25 = bf16[1,1,512,602]{3,2,1,0:T(8,128)(2,1)} copy(bf16[1,1,512,602]{2,3,1,0:T(8,128)(2,1)} %param.18) | data formatting | bytes 1232896 | tf_op args[5]
  7.7 0.0 copy-done
  7.7 1.4 %copy.24 = bf16[1,1,1024,602]{3,2,1,0:T(8,128)(2,1)} copy(bf16[1,1,1024,602]{2,3,1,0:T(8,128)(2,1)S(1)} %copy-done) | data formatting | bytes 2465792 | tf_op args[0]
  9.1 48.6 %step.1 = (bf16[2048,128]{1,0:T(8,128)(2,1)}, bf16[512,256]{1,0:T(8,128)(2,1)}, bf16[512,256]{1,0:T(8,128)(2,1)}, bf16[512,256]{1,0:T(8,128)(2,1)}, bf16[512,256]{1,0:T(8,128)(2,1)}) custom-call(s32[1024,1024]{1,0:T(8,128)} %bitcast.16, s32[1024,512]{1,0:T(8,128)} %bitcast.18, bf16[1024,602]{1,0:T(8,128)(2,1)} %bitcast.15, bf16[512,602]{1,0:T(8,128)(2,1)} %bitcast.17, ...), custom_call_target="tpu_custom_call" | custom-call | tf_op jit(solution)/shard_map/step/pallas_call | solution.py:371
  57.7 2.7 %finish.1 = (f32[602,256]{1,0:T(8,128)}, f32[256,256]{1,0:T(8,128)}, f32[256,41]{1,0:T(8,128)}, bf16[512,256]{1,0:T(8,128)(2,1)}, bf16[512,256]{1,0:T(8,128)(2,1...) custom-call(bf16[2048,128]{1,0:T(8,128)(2,1)} %get-tuple-element.19.whole, bf16[512,256]{1,0:T(8,128)(2,1)} %get-tuple-element.20.n2, ...), custom_call_target="tpu_custom_call" | custom-call | tf_op jit(solution)/shard_map/finish/pallas_call | solution.py:393
  60.4 1.6 %copy.29 = f32[256,41]{0,1:T(8,128)} copy(f32[256,41]{1,0:T(8,128)} %get-tuple-element.40) | data formatting | bytes 83968
Async XLA Ops:
  0.6 7.0 %copy-start = (bf16[1,1,1024,602]{2,3,1,0:T(8,128)(2,1)S(1)}, bf16[1,1,1024,602]{2,3,1,0:T(8,128)(2,1)}, u32[]{:S(2)}) copy-start(bf16[1,1,1024,602]{2,3,1,0:T(8,128)(2,1)} %param.13) | copy-start | bytes 3698692

commit v3 on v2

--- a/solution.py
+++ b/solution.py
@@ -207,7 +207,7 @@
 
 
 NAMES = ("local", "halo", "features", "halo_first", "halo_second", "halo_third", "return_second", "return_third",
-         "weight_first", "weight_second", "weight_third", "index_row", "index_col", "labels")
+         "weight_first", "weight_second", "weight_third", "index_row", "labels")
 
 
 def step_kernel(plan, tiles, *refs):
@@ -216,23 +216,23 @@
     whole, n2, n3, b2, b3 = refs[count:count + 5]
     held = dict(zip(NAMES, refs[count + 5:2 * count + 5]))
     (in_sem, local_bf, halo_bf, inverse, hits, hits_t, mixed_one, mixed_two, mixed_three, pre_one, pre_two, hidden_one,
-     hidden_two, scaled, upstream, upstream_three, s2, s3, o2, o3, hsend, hrecv,
-     packed, packed_bf, got_pair, got_col, got_deep, acc_bf) = refs[2 * count + 5:2 * count + 33]
-    sems = refs[2 * count + 33:]
-    nodes = held["features"].shape[0]
+     hidden_two, scaled, upstream, upstream_three, target_held, s2, s3, o2, o3, hsend, hrecv,
+     packed, packed_bf, got_pair, got_col, got_deep, acc_bf) = refs[2 * count + 5:2 * count + 34]
+    sems = refs[2 * count + 34:]
+    nodes = held["local"].shape[0]
     tall = nodes // tiles
     tile = [pl.ds(t * tall, tall) for t in range(tiles)]
     plan.place()
 
     loads = {}
-    for name in ("index_row", "index_col", "features", "halo_first", "local", "halo") + NAMES[4:11] + ("labels",):
+    for name in ("index_row", "features", "halo_first", "local", "halo") + NAMES[4:11] + ("labels",):
         if name in ("local", "halo"):
             for t in range(tiles):
                 key = (name, t)
                 loads[key] = pltpu.make_async_copy(hbm[name].at[tile[t]], held[name].at[tile[t]], in_sem.at[len(loads)])
         else:
             loads[name] = pltpu.make_async_copy(hbm[name], held[name], in_sem.at[len(loads)])
-    order = ["index_row", "index_col", "features", "halo_first"]
+    order = ["index_row", "features", "halo_first"]
     for t in range(tiles):
         order += [("local", t), ("halo", t)]
     order += [name for name in loads if name not in order]
@@ -251,27 +251,30 @@
             packed_bf[rows, :] = value[:, lanes].astype(BF)
 
     loads["index_row"].wait()
-    loads["index_col"].wait()
     slots = hits.shape[1]
     hits[...] = jnp.where(lax.broadcasted_iota(jnp.int32, (nodes, slots), 0) == held["index_row"][...], 1.0, 0.0).astype(BF)
-    hits_t[...] = jnp.where(lax.broadcasted_iota(jnp.int32, (slots, nodes), 1) == held["index_col"][...], 1.0, 0.0).astype(BF)
+    hits_t[...] = hits[...].T
+    loads["labels"].wait()
+    wide = target_held.shape[1]
+    target_held[...] = jnp.where(lax.broadcasted_iota(jnp.int32, (wide, nodes), 0) == held["labels"][...], 1.0, 0.0).T
     loads["features"].wait()
     loads["halo_first"].wait()
 
-    def spread(t, values, remote, out):
-        total = dot(local_bf[tile[t], :], values[...]) + values[tile[t], :].astype(F32) + dot(halo_bf[tile[t], :], remote[...])
+    def spread(t, values, remote, out, dims=((1,), (0,))):
+        total = dot(local_bf[tile[t], :], values[...], dims) + dot(halo_bf[tile[t], :], remote[...], dims)
         out[tile[t], :] = (total * inverse[tile[t], :]).astype(BF)
 
     for t in range(tiles):
         loads[("local", t)].wait()
         loads[("halo", t)].wait()
         near, far = held["local"][tile[t], :].astype(F32), held["halo"][tile[t], :].astype(F32)
-        local_bf[tile[t], :] = near.astype(BF)
+        here = lax.broadcasted_iota(jnp.int32, near.shape, 0) + t * tall == lax.broadcasted_iota(jnp.int32, near.shape, 1)
+        local_bf[tile[t], :] = jnp.where(here, near + 1.0, near).astype(BF)
         halo_bf[tile[t], :] = far.astype(BF)
         inverse[tile[t], :] = 1.0 / (1.0 + jnp.sum(near, axis=1, keepdims=True) + jnp.sum(far, axis=1, keepdims=True))
-        spread(t, held["features"], held["halo_first"], mixed_one)
+        spread(t, held["features"], held["halo_first"], mixed_one, ((1,), (1,)))
         if t == 0:
-            for name in NAMES[4:11] + ("labels",):
+            for name in NAMES[4:11]:
                 loads[name].wait()
         pre = dot(mixed_one[tile[t], :], held["weight_first"][...])
         pre_one[tile[t], :] = pre
@@ -287,17 +290,17 @@
     halo_start(plan, s3, n3, hsend, hrecv, 1)
     for t in range(tiles):
         spread(t, hidden_two, held["halo_third"], mixed_three)
-        logits = dot(mixed_three[tile[t], :], held["weight_third"][...])
+        logits = dot(mixed_three[tile[t], :], held["weight_third"][...], ((1,), (1,)))
         expo = jnp.exp(logits)
         probs = expo / jnp.sum(expo, axis=1, keepdims=True)
-        target = jnp.where(held["labels"][tile[t], :] == lax.broadcasted_iota(jnp.int32, logits.shape, 1), 1.0, 0.0)
+        target = target_held[tile[t], :logits.shape[1]]
         up = ((probs - target) / nodes).astype(BF)
         upstream_three[tile[t], :] = up
-        scaled[tile[t], :] = (dot(up, held["weight_third"][...], ((1,), (1,))) * inverse[tile[t], :]).astype(BF)
+        scaled[tile[t], :] = (dot(up, held["weight_third"][...]) * inverse[tile[t], :]).astype(BF)
     turn = ((0,), (0,))
 
     def carry(t, returned):
-        return dot(local_bf[:, tile[t]], scaled[...], turn) + scaled[tile[t], :].astype(F32) + dot(hits[tile[t], :], returned[...])
+        return dot(local_bf[:, tile[t]], scaled[...], turn) + dot(hits[tile[t], :], returned[...])
 
     for t in range(tiles):
         upstream[tile[t], :] = (carry(t, held["return_third"]) * slope(pre_two[tile[t], :])).astype(BF)
@@ -337,14 +340,10 @@
     copies = [pltpu.make_async_copy(src, dst, sem.at[i]) for i, (src, dst) in enumerate(((n2, m2), (n3, m3), (b2, a2), (b3, a3)))]
     for copy in copies:
         copy.start()
-    for ref, at in ((h1, plan.at_first), (h2, plan.at_second)):
+    for ref, at in ((h1, plan.at_first), (h2, plan.at_second), (h3, plan.at_third)):
         for j in range(plan.strips):
             rows, lanes = plan.strip(at, ref.shape[0], j)
             ref[:, lanes] = whole[rows, :].astype(F32)
-    classes = h3.shape[1]
-    for j in range(plan.strips):
-        rows, lanes = plan.strip(plan.at_third, up_to(classes, 16), j)
-        h3[lanes, :] = whole[rows, :].astype(F32).T[:, :classes]
     for i, (src, dst) in enumerate(((h1, g1), (h2, g2), (h3, g3))):
         copies.append(pltpu.make_async_copy(src, dst, sem.at[4 + i]))
         copies[-1].start()
@@ -362,8 +361,8 @@
     slots, hidden, classes = index.shape[0], weight_first.shape[1], weight_third.shape[1]
     plan = Plan(mesh, weight_first.shape, weight_second.shape, weight_third.shape[::-1])
     tiles = 4 if nodes % 512 == 0 else 1
-    values = (local_mask, halo_mask, features, halo_first, halo_second, halo_third, return_second, return_third,
-              weight_first, weight_second, weight_third, index[None, :], index[:, None], labels[:, None])
+    values = (local_mask, halo_mask, features.T, halo_first.T, halo_second, halo_third, return_second, return_third,
+              weight_first, weight_second, weight_third.T, index[None, :], labels[None, :])
     vmem, anywhere = pl.BlockSpec(memory_space=pltpu.VMEM), pl.BlockSpec(memory_space=pl.ANY)
     dma = pltpu.SemaphoreType.DMA
     peers, deep, n, lanes = max(plan.n_col - 1, 1), max(plan.deep - 1, 1), plan.pieces, plan.lanes
@@ -378,7 +377,8 @@
             pltpu.VMEM((nodes, width), BF), pltpu.VMEM((nodes, hidden), BF), pltpu.VMEM((nodes, hidden), BF),
             pltpu.VMEM((nodes, hidden), F32), pltpu.VMEM((nodes, hidden), F32),
             pltpu.VMEM((nodes, hidden), BF), pltpu.VMEM((nodes, hidden), BF), pltpu.VMEM((nodes, hidden), BF),
-            pltpu.VMEM((nodes, hidden), BF), pltpu.VMEM((nodes, classes), BF)]
+            pltpu.VMEM((nodes, hidden), BF), pltpu.VMEM((nodes, classes), BF),
+            pltpu.VMEM((nodes, up_to(classes, 128)), F32)]
         + [pltpu.VMEM((slots, hidden), BF)] * 4 + [dma((4, 4)), dma((4, 4)),
             pltpu.VMEM((plan.total, lanes), F32), pltpu.VMEM((plan.total, lanes), BF),
             pltpu.VMEM((n, plan.half, lanes), BF), pltpu.VMEM((n, peers, plan.quarter, lanes), BF),
@@ -389,7 +389,7 @@
         name="step",
     )(*values)
     whole, n2, n3, b2, b3 = done
-    grads = ((weight_first.shape, F32), (weight_second.shape, F32), (weight_third.shape, F32))
+    grads = ((weight_first.shape, F32), (weight_second.shape, F32), (weight_third.shape[::-1], F32))
     out = pl.pallas_call(
         functools.partial(finish_kernel, plan),
         out_shape=tuple(jax.ShapeDtypeStruct(*g) for g in grads) + (block,) * 4,
@@ -397,7 +397,7 @@
         scratch_shapes=[pltpu.VMEM(*g) for g in grads] + [dma((7,))],
         name="finish",
     )(whole, n2, n3, b2, b3)
-    return out[:3] + tuple(v[None, None] for v in out[3:])
+    return (out[0], out[1], out[2].T) + tuple(v[None, None] for v in out[3:])
 
 
 def solution(mesh):

time: 62.3 us -> 53.5 us (0.86)
  local copies, waits for them, and re-layouts: 10.1 us -> 0 us
  Pallas kernels: 51.3 us -> 52.5 us
    unnamed x6 -> x0, local copies, waits for them, and re-layouts: 6.84 us -> none
    another operation x2 -> x0, local copies, waits for them, and re-layouts: 3.24 us -> none  [the longest x1 1.71 us: per_device(): labels[:, None]]
    pallas_call x1, Pallas kernels: 48.6 us -> 49.9 us  [per_device(): pl.pallas_call(functools.partial(step_kernel, plan, tiles), out_shape=(ja...]
where the time goes in v3:
time: 53.5 us; the launch traced here: 53.3 us
  Pallas kernels  52.5 us (98%)
  between operations  0.81 us (2%)
    pallas_call x1, Pallas kernels, per_device(): pl.pallas_call(functools.partial(step_kernel, plan, tiles), out_shape=(ja...  49.9 us
    pallas_call x1, Pallas kernels, per_device(): pl.pallas_call(functools.partial(finish_kernel, plan), out_shape=tuple((j...  2.66 us

profile of v3, /device:TPU:0, one launch (start us, length us, event | category | flops | bytes accessed | tf_op | source)
XLA Modules:
  0.0 53.3 jit_solution(2743639316814240168)
XLA Ops:
  0.6 49.9 %step.1 = (bf16[2048,128]{1,0:T(8,128)(2,1)}, bf16[512,256]{1,0:T(8,128)(2,1)}, bf16[512,256]{1,0:T(8,128)(2,1)}, bf16[512,256]{1,0:T(8,128)(2,1)}, bf16[512,256]{1,0:T(8,128)(2,1)}) custom-call(s32[1024,1024]{1,0:T(8,128)} %bitcast.20, s32[1024,512]{1,0:T(8,128)} %bitcast.21, bf16[602,1024]{1,0:T(8,128)(2,1)} %bitcast.22, bf16[602,512]{1,0:T(8,128)(2,1)} %bitcast.23, ...), custom_call_target="tpu_custom_call" | custom-call | tf_op jit(solution)/shard_map/step/pallas_call | solution.py:370
  50.5 2.7 %finish.1 = (f32[602,256]{1,0:T(8,128)}, f32[256,256]{1,0:T(8,128)}, f32[41,256]{1,0:T(8,128)}, bf16[512,256]{1,0:T(8,128)(2,1)}, bf16[512,256]{1,0:T(8,128)(2,1...) custom-call(bf16[2048,128]{1,0:T(8,128)(2,1)} %get-tuple-element.19.whole, bf16[512,256]{1,0:T(8,128)(2,1)} %get-tuple-element.20.n2, ...), custom_call_target="tpu_custom_call" | custom-call | tf_op jit(solution)/shard_map/finish/pallas_call | solution.py:393
